TPU v7x, 32 devices: a whole 2x2x4 slice. The times are simulated.
32 devices in a mesh: section: 2 (over core), dp: 16 (over z, y, x).
Axes of the slice: x: 2, y: 2, z: 4, core: 2. Of those that a mesh axis runs over, the one named last changes fastest.
Arguments:
- pixels: bfloat16 [32, 196, 768], P('dp'), may hold values from -6 to 6
- ctx_idx: int32 [32, 128], P('dp'), may hold values from 0 to 195, as said below
- ctx_len: int32 [32], P('dp'), may hold values from 64 to 128
- tgt_idx: int32 [32, 4, 36], P('dp'), may hold values from 0 to 195, as said below
- tgt_len: int32 [32, 4], P('dp'), may hold values from 4 to 36, as said below
- slot_of: int32 [68], replicated, may hold values from 0 to 79, as said below
- weights: float32 [2, 80, 384, 384], P('section', 'dp')
- first_moment: float32 [2, 80, 384, 384], P('section', 'dp'), may hold values from -0.001953125 to 0.001953125
- second_moment: float32 [2, 80, 384, 384], P('section', 'dp'), may hold values from 4.9773828e-08 to 7.9638124e-07
- left_basis: float32 [2, 80, 384, 384], P('section', 'dp'), as said below
- right_basis: float32 [2, 80, 384, 384], P('section', 'dp'), as said below
- left_stats: float32 [2, 80, 384, 384], P('section', 'dp'), as said below
- right_stats: float32 [2, 80, 384, 384], P('section', 'dp'), as said below
- vectors: float32 [2, 18432], P('section')
- vector_first: float32 [2, 18432], P('section'), may hold values from -0.005859375 to 0.005859375
- vector_second: float32 [2, 18432], P('section'), may hold values from 9.9547655e-08 to 6.37105e-06
Outputs:
- loss_sum: float32 [], replicated
- loss_count: float32 [], replicated
- grad_norm: float32 [], replicated
- new_weights: float32 [2, 80, 384, 384], P('section', 'dp')
- new_first: float32 [2, 80, 384, 384], P('section', 'dp')
- new_second: float32 [2, 80, 384, 384], P('section', 'dp')
- new_left: float32 [2, 80, 384, 384], P('section', 'dp')
- new_right: float32 [2, 80, 384, 384], P('section', 'dp')
- new_left_stats: float32 [2, 80, 384, 384], P('section', 'dp')
- new_right_stats: float32 [2, 80, 384, 384], P('section', 'dp')
- new_vectors: float32 [2, 18432], P('section')
- new_vector_first: float32 [2, 18432], P('section')
- new_vector_second: float32 [2, 18432], P('section')
Inputs may be any that keep to these rules, and one draw needn't show every extreme that they name: `ctx_idx`: each image's 128 context patch numbers are distinct; the first ctx_len of them count. `tgt_idx`: each target block is a rectangle of the 14 x 14 patch grid, listed row by row; entries past its length are 0. `tgt_len`: A block's height times its width, with heights 2 to 6 and widths 2 to 6. `slot_of`: distinct slot numbers. `left_basis`: each block is orthogonal. `right_basis`: each block is orthogonal. `left_stats`: each block is symmetric positive definite. `right_stats`: each block is symmetric positive definite.
All inputs are finite; a program needn't handle non-finite values.
Results may differ from a plain program's by a relative error of at most 0.00065.
The roundings to bfloat16 on the way count: a program that leaves them out, or rounds other values in their place, can miss the bound.
Values may be sent and summed in bfloat16 or wider, within the bound.
No kernel may reach another device: no remote copies, remote signals or barrier semaphores. Data moves between devices by JAX's collectives and lax.ppermute only.
A program may use at most 384 MiB of HBM per device.

v0:
```python
import math

import jax
import jax.numpy as jnp
from jax import lax
from jax.sharding import PartitionSpec as P

D = 768
FF = 3072
H = 12
PD = 384
PFF = 1536
PH = 12
PIX = 768
GRID = 14
NT = 4
LC = 128
MB = 2
STEP = 10
IMG = 1
P_SIZE = 196
LT = 36
NBE = 52
NBP = 16
VE = 11520
VP = 6912
VW = 18432


TOP_PRECISION = lax.Precision.HIGHEST
NORM_EPS = 1e-06
ADAM_EPS = 1e-08
BETA_FIRST = 0.5
BETA_SECOND = 0.5
BETA_STATS = 0.95
RATE_MATRIX = 0.02
RATE_VECTOR = 0.05
DECAY_MATRIX = 0.04
EMA_KEEP = 0.996
CLIP_LIMIT = 1.0
NEG_FILL = -1000000000.0


def from_behind(shard, axis, by):
    size = lax.axis_size(axis)
    pairs = [(i, i + by) for i in range(size) if 0 <= i + by < size]
    return lax.ppermute(shard, axis, pairs)


def enc_shapes():
    return [(PIX, D), (D, 3 * D), (D, D), (D, FF), (FF, D)]


def pred_shapes():
    return [(D, PD), (PD, 3 * PD), (PD, PD), (PD, PFF), (PFF, PD), (PD, D)]


def enc_lengths():
    return [D] * 8 + [FF, D, D, D]


def pred_lengths():
    return [PD] * 8 + [PFF, PD, PD, PD, D, PD]


def assemble(blocks, height, breadth):
    block_edge = blocks.shape[-1]
    tiled = blocks.reshape(height // block_edge, breadth // block_edge, block_edge, block_edge)
    return tiled.transpose(0, 2, 1, 3).reshape(height, breadth)


def split_blocks(matrix, block_edge):
    height, breadth = matrix.shape
    tiled = matrix.reshape(height // block_edge, block_edge, breadth // block_edge, block_edge)
    return tiled.transpose(0, 2, 1, 3).reshape(-1, block_edge, block_edge)


def unpack_mats(blocks, shapes):
    block_edge = blocks.shape[-1]
    result = []
    offset = 0
    for height, breadth in shapes:
        amount = height * breadth // (block_edge * block_edge)
        result.append(assemble(blocks[offset : offset + amount], height, breadth))
        offset += amount
    return result


def pack_mats(matrices, block_edge):
    return jnp.concatenate([split_blocks(matrix, block_edge) for matrix in matrices], 0)


def unpack_vec(vector, lengths):
    result = []
    offset = 0
    for length in lengths:
        result.append(vector[offset : offset + length])
        offset += length
    return result


def sincos(width):
    quarter = width // 4
    frequency = 1.0 / 10000.0 ** (jnp.arange(quarter, dtype=jnp.float32) / quarter)
    cell_ids = jnp.arange(P_SIZE)
    row_pos = (cell_ids // GRID).astype(jnp.float32)[:, None] * frequency
    column_pos = (cell_ids % GRID).astype(jnp.float32)[:, None] * frequency
    return jnp.concatenate(
        [jnp.sin(row_pos), jnp.cos(row_pos), jnp.sin(column_pos), jnp.cos(column_pos)], 1
    )


def layer_norm(inputs, gain_vec, shift_vec):
    center = inputs - jnp.mean(inputs, -1, keepdims=True)
    spread = jnp.mean(center * center, -1, keepdims=True)
    return center * lax.rsqrt(spread + NORM_EPS) * gain_vec + shift_vec


def plain_norm(inputs):
    center = inputs - jnp.mean(inputs, -1, keepdims=True)
    spread = jnp.mean(center * center, -1, keepdims=True)
    return center * lax.rsqrt(spread + NORM_EPS)


def gelu_exact(inputs):
    return jax.nn.gelu(inputs, approximate=False)


def dense(left_op, right_op):
    return jnp.einsum("...k,km->...m", left_op, right_op, preferred_element_type=jnp.float32)


def dense_back(inputs, weight, grad_out):
    grad_low = grad_out.astype(jnp.bfloat16)
    grad_in = jnp.einsum("...m,km->...k", grad_low, weight, preferred_element_type=jnp.float32)
    grad_weight = jnp.einsum("...k,...m->km", inputs, grad_low, preferred_element_type=jnp.float32)
    return (grad_in, grad_weight)


def lead_sum(values):
    return jnp.sum(values.reshape(-1, values.shape[-1]), 0)


def attend_forward(qkv, valid, heads):
    batch_size, length, triple = qkv.shape
    model_width = triple // 3
    head_dim = model_width // heads
    split_shape = (batch_size, length, heads, head_dim)
    queries = (
        (qkv[..., :model_width] * (1.0 / math.sqrt(head_dim)))
        .astype(jnp.bfloat16)
        .reshape(split_shape)
    )
    keys_low = qkv[..., model_width : 2 * model_width].astype(jnp.bfloat16).reshape(split_shape)
    values_low = qkv[..., 2 * model_width :].astype(jnp.bfloat16).reshape(split_shape)
    scores = jnp.einsum("nqhd,nkhd->nhqk", queries, keys_low, preferred_element_type=jnp.float32)
    scores = jnp.where(valid[:, None, None, :], scores, NEG_FILL)
    softmax_out = jax.nn.softmax(scores, axis=-1)
    softmax_low = softmax_out.astype(jnp.bfloat16)
    attended = jnp.einsum(
        "nhqk,nkhd->nqhd", softmax_low, values_low, preferred_element_type=jnp.float32
    )
    return (
        attended.reshape(batch_size, length, model_width),
        (queries, keys_low, values_low, softmax_out, softmax_low),
    )


def attend_backward(kept, grad_out):
    queries, keys_low, values_low, softmax_out, softmax_low = kept
    batch_size, length, heads, head_dim = queries.shape
    grad_low = grad_out.astype(jnp.bfloat16).reshape(batch_size, length, heads, head_dim)
    grad_values = jnp.einsum(
        "nhqk,nqhd->nkhd", softmax_low, grad_low, preferred_element_type=jnp.float32
    )
    grad_probs = jnp.einsum(
        "nqhd,nkhd->nhqk", grad_low, values_low, preferred_element_type=jnp.float32
    )
    grad_scores = softmax_out * (grad_probs - jnp.sum(grad_probs * softmax_out, -1, keepdims=True))
    scores_low = grad_scores.astype(jnp.bfloat16)
    grad_queries = jnp.einsum(
        "nhqk,nkhd->nqhd", scores_low, keys_low, preferred_element_type=jnp.float32
    ) * (1.0 / math.sqrt(head_dim))
    grad_keys = jnp.einsum(
        "nhqk,nqhd->nkhd", scores_low, queries, preferred_element_type=jnp.float32
    )
    flat_shape = (batch_size, length, heads * head_dim)
    return jnp.concatenate(
        [
            grad_queries.reshape(flat_shape),
            grad_keys.reshape(flat_shape),
            grad_values.reshape(flat_shape),
        ],
        -1,
    )


def block_forward(inputs, valid, matrices, vector_list, heads):
    weight_proj, weight_out, weight_up, weight_down = matrices
    (
        gain_one,
        shift_one,
        bias_query,
        bias_value,
        bias_output,
        gain_two,
        shift_two,
        bias_up,
        bias_down,
    ) = vector_list
    bias_all = jnp.concatenate([bias_query, jnp.zeros_like(bias_query), bias_value])
    normed_low = layer_norm(inputs, gain_one, shift_one).astype(jnp.bfloat16)
    qkv = dense(normed_low, weight_proj) + bias_all
    attended, attn_kept = attend_forward(qkv, valid, heads)
    attended_low = attended.astype(jnp.bfloat16)
    middle = inputs + dense(attended_low, weight_out) + bias_output
    hidden_low = layer_norm(middle, gain_two, shift_two).astype(jnp.bfloat16)
    pre_act = dense(hidden_low, weight_up) + bias_up
    act_low = gelu_exact(pre_act).astype(jnp.bfloat16)
    output = middle + dense(act_low, weight_down) + bias_down
    return (
        output,
        (inputs, normed_low, attn_kept, attended_low, middle, hidden_low, pre_act, act_low),
    )


def block_backward(kept, grad_out, matrices, vector_list):
    inputs, normed_low, attn_kept, attended_low, middle, hidden_low, pre_act, act_low = kept
    weight_proj, weight_out, weight_up, weight_down = matrices
    (
        gain_one,
        shift_one,
        bias_query,
        bias_value,
        bias_output,
        gain_two,
        shift_two,
        bias_up,
        bias_down,
    ) = vector_list
    grad_act, grad_down = dense_back(act_low, weight_down, grad_out)
    grad_pre = jax.vjp(gelu_exact, pre_act)[1](grad_act)[0]
    grad_hidden, grad_up = dense_back(hidden_low, weight_up, grad_pre)
    grad_middle, grad_gain_two, grad_shift_two = jax.vjp(layer_norm, middle, gain_two, shift_two)[
        1
    ](grad_hidden)
    grad_middle = grad_middle + grad_out
    grad_attn, grad_output = dense_back(attended_low, weight_out, grad_middle)
    grad_qkv = attend_backward(attn_kept, grad_attn)
    bias_sums = lead_sum(grad_qkv)
    model_width = inputs.shape[-1]
    grad_normed, grad_proj = dense_back(normed_low, weight_proj, grad_qkv)
    grad_inputs, grad_gain_one, grad_shift_one = jax.vjp(layer_norm, inputs, gain_one, shift_one)[
        1
    ](grad_normed)
    mats_out = [grad_proj, grad_output, grad_up, grad_down]
    vecs_out = [
        grad_gain_one,
        grad_shift_one,
        bias_sums[:model_width],
        bias_sums[2 * model_width :],
        lead_sum(grad_middle),
        grad_gain_two,
        grad_shift_two,
        lead_sum(grad_pre),
        lead_sum(grad_out),
    ]
    return (grad_inputs + grad_middle, mats_out, vecs_out)


def encode_forward(pixel_rows, position, valid, matrices, vector_list):
    embedded = dense(pixel_rows, matrices[0]) + vector_list[0] + position
    hidden, saved = block_forward(embedded, valid, matrices[1:], vector_list[1:10], H)
    return (layer_norm(hidden, vector_list[10], vector_list[11]), (hidden, saved))


def encode_backward(pixel_rows, kept, grad_out, matrices, vector_list):
    hidden, saved = kept
    grad_hidden, grad_gain, grad_shift = jax.vjp(
        layer_norm, hidden, vector_list[10], vector_list[11]
    )[1](grad_out)
    grad_embed, layer_mats, layer_vecs = block_backward(
        saved, grad_hidden, matrices[1:], vector_list[1:10]
    )
    grad_patch = jnp.einsum(
        "...k,...m->km",
        pixel_rows,
        grad_embed.astype(jnp.bfloat16),
        preferred_element_type=jnp.float32,
    )
    return (
        [grad_patch] + layer_mats,
        [lead_sum(grad_embed)] + layer_vecs + [grad_gain, grad_shift],
    )


def target_forward(pixel_all, tgt_rows, position, matrices, vector_list):
    all_valid = jnp.ones(pixel_all.shape[:2], jnp.bool_)
    encoded, _ = encode_forward(pixel_all, position, all_valid, matrices, vector_list)
    return jnp.take_along_axis(plain_norm(encoded), tgt_rows[:, :, None], 1)


def predict_forward(context, ctx_pos, tgt_pos, valid, matrices, vector_list):
    entry = dense(context, matrices[0]) + vector_list[0] + ctx_pos
    joined = jnp.concatenate([entry, vector_list[13] + tgt_pos], 1)
    hidden, saved = block_forward(joined, valid, matrices[1:5], vector_list[1:10], PH)
    tail = hidden[:, LC:]
    normed = layer_norm(tail, vector_list[10], vector_list[11]).astype(jnp.bfloat16)
    return (dense(normed, matrices[5]) + vector_list[12], (saved, tail, normed))


def predict_backward(context, kept, grad_out, matrices, vector_list):
    saved, tail, normed = kept
    grad_normed, grad_final = dense_back(normed, matrices[5], grad_out)
    grad_tail, grad_gain, grad_shift = jax.vjp(layer_norm, tail, vector_list[10], vector_list[11])[
        1
    ](grad_normed)
    grad_hidden = jnp.concatenate(
        [jnp.zeros((tail.shape[0], LC, tail.shape[2]), jnp.float32), grad_tail], 1
    )
    grad_joined, layer_mats, layer_vecs = block_backward(
        saved, grad_hidden, matrices[1:5], vector_list[1:10]
    )
    grad_entry = grad_joined[:, :LC]
    grad_queries = grad_joined[:, LC:]
    grad_context, grad_first = dense_back(context, matrices[0], grad_entry)
    mats_out = [grad_first] + layer_mats + [grad_final]
    vecs_out = (
        [lead_sum(grad_entry)]
        + layer_vecs
        + [grad_gain, grad_shift, lead_sum(grad_out), lead_sum(grad_queries)]
    )
    return (grad_context, mats_out, vecs_out)


def mul(left_op, right_op):
    return jnp.dot(left_op, right_op, precision=TOP_PRECISION)


def orthonormal(matrix):
    factor = jnp.linalg.cholesky(mul(matrix.T, matrix))
    return jax.scipy.linalg.solve_triangular(factor, matrix.T, lower=True).T


def soap_update(weight, gradient, moment, second, left_op, right_op, left_stat, right_stat):
    correct_one = 1.0 - BETA_FIRST**STEP
    correct_two = 1.0 - BETA_SECOND**STEP
    rotated = mul(mul(left_op.T, gradient), right_op)
    moment_new = BETA_FIRST * moment + (1.0 - BETA_FIRST) * rotated
    second_new = BETA_SECOND * second + (1.0 - BETA_SECOND) * rotated * rotated
    normed = moment_new / correct_one / (jnp.sqrt(second_new / correct_two) + ADAM_EPS)
    weight_new = weight - RATE_MATRIX * (
        mul(mul(left_op, normed), right_op.T) + DECAY_MATRIX * weight
    )
    left_stat_new = BETA_STATS * left_stat + (1.0 - BETA_STATS) * mul(gradient, gradient.T)
    right_stat_new = BETA_STATS * right_stat + (1.0 - BETA_STATS) * mul(gradient.T, gradient)
    left_new = orthonormal(mul(left_stat_new, left_op))
    right_new = orthonormal(mul(right_stat_new, right_op))
    moment_out = mul(mul(mul(left_new.T, left_op), moment_new), mul(right_op.T, right_new))
    return (weight_new, moment_out, second_new, left_new, right_new, left_stat_new, right_stat_new)


def zero_mats(shapes):
    return [jnp.zeros(shape, jnp.float32) for shape in shapes]


def on_device(
    pixels,
    ctx_idx,
    ctx_len,
    tgt_idx,
    tgt_len,
    slot_of,
    weights,
    first_moment,
    second_moment,
    left_basis,
    right_basis,
    left_stats,
    right_stats,
    vectors,
    vector_first,
    vector_second,
):
    section_index = lax.axis_index("section")
    owner_index = lax.axis_index("dp")
    is_first = section_index == 0
    slot_count = weights.shape[1]
    block_edge = weights.shape[-1]
    slot_rows = slot_count * lax.axis_size("dp")
    gathered = lax.all_gather(weights[0].astype(jnp.bfloat16), "dp", axis=0, tiled=True)
    enc_slots = slot_of[:NBE]
    pred_slots = slot_of[NBE:]
    enc_mats = unpack_mats(jnp.take(gathered, enc_slots, 0), enc_shapes())
    pred_mats = unpack_mats(jnp.take(gathered, pred_slots, 0), pred_shapes())
    row_now = vectors[0]
    enc_vectors = unpack_vec(
        lax.dynamic_slice_in_dim(row_now, section_index * VP, VE), enc_lengths()
    )
    pred_vectors = unpack_vec(row_now[:VP], pred_lengths())
    pos_enc = sincos(D)
    pos_pred = sincos(PD)
    local_images = ctx_idx.shape[0]
    ctx_valid = jnp.arange(LC)[None, :] < ctx_len[:, None]
    tgt_flat = tgt_idx.reshape(local_images, NT * LT)
    tgt_valid = (jnp.arange(LT)[None, None, :] < tgt_len[:, :, None]).reshape(local_images, NT * LT)
    contexts = []
    targets = []
    for micro_index in range(MB):
        window = slice(micro_index * IMG, (micro_index + 1) * IMG)
        pixel_rows = jnp.take_along_axis(pixels[window], ctx_idx[window][:, :, None], 1)

        def run_encoder(unused):
            encoded, _ = encode_forward(
                pixel_rows,
                jnp.take(pos_enc, ctx_idx[window], 0),
                ctx_valid[window],
                enc_mats,
                enc_vectors,
            )
            return encoded.astype(jnp.bfloat16)

        def skip_encoder(unused):
            return jnp.zeros((IMG, LC, D), jnp.bfloat16)

        outgoing = lax.cond(is_first, run_encoder, skip_encoder, 0)
        contexts.append(from_behind(outgoing, "section", 1))

        def run_target(unused):
            return target_forward(
                pixels[window], tgt_flat[window], pos_enc[None], enc_mats, enc_vectors
            )

        def skip_target(unused):
            return jnp.zeros((IMG, NT * LT, D), jnp.float32)

        targets.append(lax.cond(is_first, skip_target, run_target, 0))
    enc_acc = zero_mats(enc_shapes())
    pred_acc = zero_mats(pred_shapes())
    vec_grads = jnp.zeros((VW,), jnp.float32)
    loss_local = jnp.zeros((), jnp.float32)
    for micro_index in reversed(range(MB)):
        window = slice(micro_index * IMG, (micro_index + 1) * IMG)
        pixel_rows = jnp.take_along_axis(pixels[window], ctx_idx[window][:, :, None], 1)
        joined_valid = jnp.concatenate([ctx_valid[window], tgt_valid[window]], 1)
        target_mask = tgt_valid[window].astype(jnp.float32)[:, :, None]

        def run_predictor(unused):
            context = contexts[micro_index]
            predicted, kept = predict_forward(
                context,
                jnp.take(pos_pred, ctx_idx[window], 0),
                jnp.take(pos_pred, tgt_flat[window], 0),
                joined_valid,
                pred_mats,
                pred_vectors,
            )
            difference = predicted - targets[micro_index]
            magnitude = jnp.abs(difference)
            loss_value = jnp.sum(
                jnp.where(magnitude < 1.0, 0.5 * difference * difference, magnitude - 0.5)
                * target_mask
            )
            grad_out = jnp.clip(difference, -1.0, 1.0) * target_mask
            grad_context, mats_grad, vecs_grad = predict_backward(
                context, kept, grad_out, pred_mats, pred_vectors
            )
            return (
                grad_context.astype(jnp.bfloat16),
                mats_grad,
                jnp.concatenate(vecs_grad),
                loss_value,
            )

        def skip_predictor(unused):
            return (
                jnp.zeros((IMG, LC, D), jnp.bfloat16),
                zero_mats(pred_shapes()),
                jnp.zeros((VP,), jnp.float32),
                jnp.zeros((), jnp.float32),
            )

        back_send, pred_part, pred_vec_part, loss_part = lax.cond(
            is_first, skip_predictor, run_predictor, 0
        )
        incoming = from_behind(back_send, "section", -1)

        def run_encoder_back(unused):
            encoded, kept = encode_forward(
                pixel_rows,
                jnp.take(pos_enc, ctx_idx[window], 0),
                ctx_valid[window],
                enc_mats,
                enc_vectors,
            )
            mats_grad, vecs_grad = encode_backward(
                pixel_rows, kept, incoming.astype(jnp.float32), enc_mats, enc_vectors
            )
            return (mats_grad, jnp.concatenate(vecs_grad))

        def skip_encoder_back(unused):
            return (zero_mats(enc_shapes()), jnp.zeros((VE,), jnp.float32))

        enc_part, enc_vec_part = lax.cond(is_first, run_encoder_back, skip_encoder_back, 0)
        vec_grads = (
            vec_grads + jnp.pad(enc_vec_part, (0, VW - VE)) + jnp.pad(pred_vec_part, (0, VW - VP))
        )
        loss_local = loss_local + loss_part
        enc_acc = [total + part for total, part in zip(enc_acc, enc_part)]
        pred_acc = [total + part for total, part in zip(pred_acc, pred_part)]
    count_local = jnp.where(is_first, 0, jnp.sum(tgt_len)).astype(jnp.float32)
    loss_total, count_total = lax.psum((loss_local, count_local), ("section", "dp"))
    enc_grads = pack_mats(enc_acc, block_edge)
    pred_grads = pack_mats(pred_acc, block_edge)
    entry_count = block_edge * block_edge
    padded_pred = jnp.pad(pred_grads, ((0, NBE - NBP), (0, 0), (0, 0)))
    section_rows = jnp.where(is_first, enc_grads, padded_pred).reshape(NBE, entry_count)
    column_part = lax.psum_scatter(section_rows, "dp", scatter_dimension=1, tiled=True)
    spare_slots = jnp.full((NBE - NBP,), slot_rows, jnp.int32)
    destination = jnp.where(is_first, enc_slots, jnp.concatenate([pred_slots, spare_slots]))
    placed = (
        jnp.zeros((slot_rows, column_part.shape[1]), jnp.float32)
        .at[destination]
        .add(column_part, mode="drop")
    )
    owned_sum = lax.all_to_all(placed, "dp", split_axis=0, concat_axis=1, tiled=True).reshape(
        slot_count, block_edge, block_edge
    )
    vec_total = lax.psum(vec_grads, "dp")
    own_ids = owner_index * slot_count + jnp.arange(slot_count)
    enc_here = jnp.any(own_ids[:, None] == enc_slots[None, :], 1)
    pred_here = jnp.any(own_ids[:, None] == pred_slots[None, :], 1)
    trained = jnp.where(is_first, enc_here, pred_here)
    ema_here = jnp.logical_and(jnp.logical_not(is_first), enc_here)
    positions = jnp.arange(VW)
    vec_trained = positions < jnp.where(is_first, VE, VP)
    vec_ema = jnp.logical_and(jnp.logical_not(is_first), positions >= VP)
    block_squares = jnp.sum(jnp.where(trained[:, None, None], owned_sum * owned_sum, 0.0))
    vec_squares = jnp.where(
        owner_index == 0, jnp.sum(jnp.where(vec_trained, vec_total * vec_total, 0.0)), 0.0
    )
    squares = block_squares + vec_squares
    square_total = lax.psum(squares, ("section", "dp"))
    grad_norm = jnp.sqrt(square_total) / count_total
    factor = jnp.minimum(1.0, CLIP_LIMIT / (grad_norm + 1e-06)) / count_total
    olds = (
        weights[0],
        first_moment[0],
        second_moment[0],
        left_basis[0],
        right_basis[0],
        left_stats[0],
        right_stats[0],
    )
    results = jax.vmap(soap_update)(
        olds[0], owned_sum * factor, olds[1], olds[2], olds[3], olds[4], olds[5], olds[6]
    )
    updated = [
        jnp.where(trained[:, None, None], fresh, stale) for fresh, stale in zip(results, olds)
    ]
    correct_one = 1.0 - BETA_FIRST**STEP
    correct_two = 1.0 - BETA_SECOND**STEP
    vec_clipped = vec_total * factor
    fresh_first = BETA_FIRST * vector_first[0] + (1.0 - BETA_FIRST) * vec_clipped
    fresh_second = BETA_SECOND * vector_second[0] + (1.0 - BETA_SECOND) * vec_clipped * vec_clipped
    stepped = row_now - RATE_VECTOR * (fresh_first / correct_one) / (
        jnp.sqrt(fresh_second / correct_two) + ADAM_EPS
    )
    new_vec = jnp.where(vec_trained, stepped, row_now)
    new_vec_first = jnp.where(vec_trained, fresh_first, vector_first[0])
    new_vec_second = jnp.where(vec_trained, fresh_second, vector_second[0])
    from_encoder, vec_from_encoder = (
        from_behind(updated[0].astype(jnp.bfloat16), "section", 1).astype(jnp.float32),
        from_behind(new_vec.astype(jnp.bfloat16), "section", 1).astype(new_vec.dtype),
    )
    updated[0] = jnp.where(
        ema_here[:, None, None], EMA_KEEP * weights[0] + (1.0 - EMA_KEEP) * from_encoder, updated[0]
    )
    aligned = jnp.concatenate([jnp.zeros((VP,), jnp.float32), vec_from_encoder[:VE]])
    new_vec = jnp.where(vec_ema, EMA_KEEP * row_now + (1.0 - EMA_KEEP) * aligned, new_vec)
    return (
        loss_total,
        count_total,
        grad_norm,
        updated[0][None],
        updated[1][None],
        updated[2][None],
        updated[3][None],
        updated[4][None],
        updated[5][None],
        updated[6][None],
        new_vec[None],
        new_vec_first[None],
        new_vec_second[None],
    )


def solution(mesh):
    in_specs = (
        P("dp", None, None),
        P("dp", None),
        P("dp"),
        P("dp", None, None),
        P("dp", None),
        P(),
        P("section", "dp", None, None),
        P("section", "dp", None, None),
        P("section", "dp", None, None),
        P("section", "dp", None, None),
        P("section", "dp", None, None),
        P("section", "dp", None, None),
        P("section", "dp", None, None),
        P("section", None),
        P("section", None),
        P("section", None),
    )
    out_specs = (
        P(),
        P(),
        P(),
        P("section", "dp", None, None),
        P("section", "dp", None, None),
        P("section", "dp", None, None),
        P("section", "dp", None, None),
        P("section", "dp", None, None),
        P("section", "dp", None, None),
        P("section", "dp", None, None),
        P("section", None),
        P("section", None),
        P("section", None),
    )
    return jax.shard_map(
        on_device, mesh=mesh, in_specs=in_specs, out_specs=out_specs, check_vma=False
    )
```

profile of v0, /device:TPU:4, one launch (start us, length us, event | category | flops | bytes accessed | tf_op | source)
XLA Modules:
  0.0 2836.5 jit_solution(10757751613135501801)
XLA Ops:
  22.5 246.5 %all-gather.2.cloned.1.call-done = bf16[80,384,384]{2,1,0:T(8,128)(2,1)} async-done(((bf16[5,384,384]{2,1,0:T(8,128)(2,1)}), bf16[80,384,384]{2,1,0:T(8,128)(2,1)}) %all-gather.2.cloned.1.call-update) | async-done | bytes 23592976 | tf_op jit(solution)/shard_map/all_gather | solution.py:391
  268.9 15.7 gather_fusion.10
  284.6 11.6 broadcast_select_fusion
  296.2 9.0 fusion.841
  312.2 11.2 gather_fusion.11
  336.9 9.8 copy.853
  354.9 11.9 copy.850
  371.3 34.7 %conditional.11 = (bf16[1,128,768]{2,1,0:T(8,128)(2,1)}) conditional(s32[]{:T(128)} %convert_element_type.534, () %tuple.85, (bf16[1,128,768]{2,1,0:T(8,128)(2,1)S(1)}, bf16[768,768]{1,0:T(8,128)(2,1)S(1)}, f32[768]{0:T(1024)S(1)}, s32[2,128]{1,0:T(2,128)S(1)}, f32[196,768]{1,0:T(8,128)S(1)}, /*index=5*/f32[768]{0:T(1024)S(1)}, ...), branch_computations={%region_53.59_spmd, %region_54.68_spmd} | conditional | flops 2069996288 | bytes 31364932 | solution.py:426
  393.4 9.4 fusion.802
  415.7 6.5 conditional.9
  422.3 36.5 %conditional.8 = (bf16[1,128,768]{2,1,0:T(8,128)(2,1)}) conditional(s32[]{:T(128)} %convert_element_type.534, () %tuple.79, (bf16[1,128,768]{2,1,0:T(8,128)(2,1)S(1)}, bf16[768,768]{1,0:T(8,128)(2,1)S(1)}, f32[768]{0:T(1024)S(1)}, s32[2,128]{1,0:T(2,128)}, f32[196,768]{1,0:T(8,128)S(1)}, /*index=5*/f32[768]{0:T(1024)S(1)}, f32[768]{0:T(1024)S(1)}, ...), branch_computations={%region_0.0_spmd, %region_1.12_spmd} | conditional | flops 2069996288 | bytes 31414652 | solution.py:426
  446.3 9.4 fusion.794
  462.4 11.1 conditional.13
  475.6 18.6 conditional.10
  535.4 117.2 %collective-permute-done.3 = bf16[1,128,768]{2,1,0:T(8,128)(2,1)} collective-permute-done((bf16[1,128,768]{2,1,0:T(8,128)(2,1)S(1)}, bf16[1,128,768]{2,1,0:T(8,128)(2,1)}, u32[]{:S(2)}, u32[]{:S(2)}) %collective-permute-start.3) | collective-permute-done | bytes 196640 | tf_op jit(solution)/shard_map/ppermute | solution.py:47
  652.7 77.8 %conditional.15 = (f32[768,768]{0,1:T(8,128)S(1)}, f32[768,2304]{1,0:T(8,128)S(1)}, f32[768,768]{1,0:T(8,128)S(1)}, f32[768,3072]{1,0:T(8,128)S(1)}, f32[3072,768]{1,0:T(8,128)S(1)}, /*index=5*/f32[18432]{0:T(1024)S(1)}) conditional(s32[]{:T(128)} %convert_element_type.534, () %tuple.92, (bf16[1,128,768]{2,1,0:T(8,128)(2,1)S(1)}, ...), branch_computations={%region_139.145_spmd, %region_140.172_spmd} | conditional | flops 5990448128 | bytes 171700976 | solution.py:504
  674.6 6.1 multiply_convert_fusion.2
  740.7 57.7 %conditional.14 = (f32[768,768]{0,1:T(8,128)}, f32[768,2304]{1,0:T(8,128)}, f32[768,768]{1,0:T(8,128)}, f32[768,3072]{1,0:T(8,128)}, f32[3072,768]{1,0:T(8,128)}, /*index=5*/f32[18432]{0:T(1024)S(1)}) conditional(s32[]{:T(128)} %convert_element_type.534, () %tuple.90, (bf16[1,128,768]{2,1,0:T(8,128)(2,1)S(1)}, bf16[768,768]{1,0:T(8,128)(2,1)S(1)}, ...), branch_computations={%region_111.117_spmd, %region_112.144_spmd} | conditional | flops 5990448128 | bytes 159129232 | solution.py:504
  752.1 6.4 multiply_convert_fusion
  798.4 12.8 add.1223
  821.2 9.2 copy.877
  841.3 8.8 add.1221
  850.1 8.0 copy.874
  858.1 9.5 reshape.3688
  867.6 13.4 copy.875
  897.5 11.1 add.1224
  908.7 12.4 reshape.3929
  921.1 8.5 copy.1000
  929.6 6.5 constant_dynamic-update-slice_fusion.51
  942.6 8.4 constant_dynamic-update-slice_fusion.48
  951.0 21.6 pad_select_fusion
  972.6 12.3 pad.135
  984.9 36.1 %copy.1043 = f32[7,8,384,384]{3,1,2,0:T(8,128)} copy(f32[7,8,384,384]{3,2,1,0:T(8,128)S(1)} %bitcast.1144) | data formatting | bytes 66060288
  1021.7 486.6 %reduce-scatter.2.cloned.1.call-done = f32[52,9216]{1,0:T(8,128)} async-done(((f32[52,147456]{1,0:T(8,128)}), f32[52,9216]{1,0:T(8,128)}) %reduce-scatter.2.cloned.1.call-update) | async-done | bytes 1916944 | tf_op jit(solution)/shard_map/reduce_scatter | solution.py:518
  1527.4 156.9 %all-reduce.17.cloned.1.call-done = f32[18432]{0:T(1024)} async-done(((f32[18432]{0:T(1024)}), f32[18432]{0:T(1024)}) %all-reduce.17.cloned.1.call-update) | async-done | bytes 73744 | tf_op jit(solution)/shard_map/psum | solution.py:529
  1691.4 40.2 %all-reduce.14 = (f32[]{:T(128)}, f32[]{:T(128)}, f32[]{:T(128)}) all-reduce(f32[]{:T(128)S(6)} %add.1216, f32[]{:T(128)S(6)} %convert_element_type.542, f32[]{:T(128)S(6)} %add.1234), channel_id=1, replica_groups=mesh['section'=2,'dp'=16] {'section','dp'}, use_global_device_ids=true, to_apply=%region_106.112 | all-reduce | flops 3 | bytes 24 | tf_op jit(solution)/shard_map/psum | solution.py:512
  1744.0 9.1 fusion.848
  1753.2 8.2 fusion.850
  1761.4 6.1 fusion.664
  1769.1 8.2 fusion.849
  1786.6 58.6 %custom-call.26 = f32[5,128,128]{2,1,0:T(8,128)S(1)} custom-call(f32[5,128,128]{2,1,0:T(8,128)S(1)} %cholesky.314), custom_call_target="Cholesky" | custom-call | tf_op jit(solution)/shard_map/vmap(jit(cholesky))/cholesky | solution.py:341
  1845.3 9.8 fusion.656
  1856.7 8.0 fusion.851
  1874.1 58.6 %custom-call.32 = f32[5,128,128]{2,1,0:T(8,128)S(1)} custom-call(f32[5,128,128]{2,1,0:T(8,128)S(1)} %cholesky.322), custom_call_target="Cholesky" | custom-call | tf_op jit(solution)/shard_map/vmap(jit(cholesky))/cholesky | solution.py:341
  1934.5 49.3 %custom-call.27 = f32[5,1,128,128]{2,3,1,0:T(8,128)S(1)} custom-call(f32[5,1,128,128]{3,2,1,0:T(8,128)S(1)} %get-tuple-element.2160), custom_call_target="InvertDiagBlocksLowerTriangular" | custom-call | tf_op jit(solution)/shard_map/vmap(jit(cholesky))/cholesky | solution.py:341
  1988.4 58.6 %custom-call.28 = f32[5,128,128]{2,1,0:T(8,128)S(1)} custom-call(f32[5,128,128]{2,1,0:T(8,128)S(1)} %cholesky.318), custom_call_target="Cholesky" | custom-call | tf_op jit(solution)/shard_map/vmap(jit(cholesky))/cholesky | solution.py:341
  2047.0 49.1 %custom-call.33 = f32[5,1,128,128]{2,3,1,0:T(8,128)S(1)} custom-call(f32[5,1,128,128]{3,2,1,0:T(8,128)S(1)} %get-tuple-element.2159), custom_call_target="InvertDiagBlocksLowerTriangular" | custom-call | tf_op jit(solution)/shard_map/vmap(jit(cholesky))/cholesky | solution.py:341
  2102.5 58.8 %custom-call.34 = f32[5,128,128]{2,1,0:T(8,128)S(1)} custom-call(f32[5,128,128]{2,1,0:T(8,128)S(1)} %cholesky.326), custom_call_target="Cholesky" | custom-call | tf_op jit(solution)/shard_map/vmap(jit(cholesky))/cholesky | solution.py:341
  2162.4 49.9 %custom-call.35 = f32[5,1,128,128]{2,3,1,0:T(8,128)S(1)} custom-call(f32[5,1,128,128]{3,2,1,0:T(8,128)} %get-tuple-element.2149), custom_call_target="InvertDiagBlocksLowerTriangular" | custom-call | tf_op jit(solution)/shard_map/vmap(jit(cholesky))/cholesky | solution.py:341
  2215.7 58.6 %custom-call.36 = f32[5,128,128]{2,1,0:T(8,128)S(1)} custom-call(f32[5,128,128]{2,1,0:T(8,128)S(1)} %convolution_subtract_fusion.4), custom_call_target="Cholesky" | custom-call | tf_op jit(solution)/shard_map/vmap(jit(cholesky))/cholesky | solution.py:341
  2274.3 49.5 %custom-call.29 = f32[5,1,128,128]{2,3,1,0:T(8,128)S(1)} custom-call(f32[5,1,128,128]{3,2,1,0:T(8,128)S(1)} %get-tuple-element.2158), custom_call_target="InvertDiagBlocksLowerTriangular" | custom-call | tf_op jit(solution)/shard_map/vmap(jit(cholesky))/cholesky | solution.py:341
  2327.2 58.6 %custom-call.30 = f32[5,128,128]{2,1,0:T(8,128)S(1)} custom-call(f32[5,128,128]{2,1,0:T(8,128)S(1)} %convolution_subtract_fusion.5), custom_call_target="Cholesky" | custom-call | tf_op jit(solution)/shard_map/vmap(jit(cholesky))/cholesky | solution.py:341
  2393.8 9.4 while.5
  2403.2 147.6 %custom-call.37 = f32[5,3,128,128]{2,3,1,0:T(8,128)S(1)} custom-call(f32[5,3,128,128]{3,2,1,0:T(8,128)S(1)} %bitcast.1274), custom_call_target="InvertDiagBlocksLowerTriangular" | custom-call | tf_op jit(solution)/shard_map/vmap(jit(_solve_triangular))/triangular_solve | solution.py:342
  2567.3 9.4 while.4
  2576.7 147.8 %custom-call.31 = f32[5,3,128,128]{2,3,1,0:T(8,128)S(1)} custom-call(f32[5,3,128,128]{3,2,1,0:T(8,128)S(1)} %bitcast.1273), custom_call_target="InvertDiagBlocksLowerTriangular" | custom-call | tf_op jit(solution)/shard_map/vmap(jit(_solve_triangular))/triangular_solve | solution.py:342
  2740.0 9.5 fusion.668
  2762.1 6.9 fusion.662
  2769.0 6.1 fusion.700
  2775.1 8.2 fusion.666
  2783.3 8.0 fusion.684
  2792.9 6.4 fusion.654
  2799.4 7.7 fusion.670
  2808.9 19.7 fusion.649
  (710 shorter events, 496.8 us)
Async XLA Ops:
  7.2 261.7 %all-gather.2.cloned.1.call-start = ((), (), s32[]{:S(2)}) async-start(), calls=%async_computation.2 | async-start | bytes 25067520 | tf_op jit(solution)/shard_map/all_gather | solution.py:391
  10.4 1497.9 %reduce-scatter.2.cloned.1.call-start = ((), (), s32[]{:S(2)}) async-start(), calls=%async_computation.3 | async-start | bytes 35094528 | tf_op jit(solution)/shard_map/reduce_scatter | solution.py:518
  10.5 405.1 %copy-start.205 = (s32[2,144]{1,0:T(2,128)}, s32[2,144]{1,0:T(2,128)S(1)}, u32[]{:S(2)}) copy-start(s32[2,144]{1,0:T(2,128)S(1)} %reshape.3679) | copy-start | bytes 3460
  14.3 357.0 %copy-start.206 = (pred[2,128]{1,0:T(4,128)(4,1)}, pred[2,128]{1,0:T(4,128)(4,1)S(1)}, u32[]{:S(2)}) copy-start(pred[2,128]{1,0:T(4,128)(4,1)S(1)} %iota_compare_fusion.6) | copy-start | bytes 772
  17.5 404.7 %copy-start.167 = (f32[768]{0:T(1024)}, f32[768]{0:T(1024)S(1)}, u32[]{:S(2)}) copy-start(f32[768]{0:T(1024)S(1)} %get-tuple-element.1893) | copy-start | bytes 9220
  17.5 404.7 %copy-start.192 = (f32[768]{0:T(1024)}, f32[768]{0:T(1024)S(1)}, u32[]{:S(2)}) copy-start(f32[768]{0:T(1024)S(1)} %get-tuple-element.1894) | copy-start | bytes 9220
  21.8 400.5 %copy-start.113 = (bf16[1,128,768]{2,1,0:T(8,128)(2,1)}, bf16[1,128,768]{2,1,0:T(8,128)(2,1)S(1)}, u32[]{:S(2)}) copy-start(bf16[1,128,768]{2,1,0:T(8,128)(2,1)S(1)} %bitcast_select_fusion.17) | copy-start | bytes 589828
  323.3 7.4 slice-start.11
  323.3 7.4 slice-start.12
  405.9 56.4 %collective-permute-start.1 = (bf16[1,128,768]{2,1,0:T(8,128)(2,1)}, bf16[1,128,768]{2,1,0:T(8,128)(2,1)}, u32[]{:S(2)}, u32[]{:S(2)}) collective-permute-start(bf16[1,128,768]{2,1,0:T(8,128)(2,1)} %get-tuple-element.2363), channel_id=1, source_target_pairs={{0,16},{1,17},{2,18},{3,19},{4,20},{5,21},{6,22},{7,23},{8,24},{9,... | collective-permute-start | bytes 589832 | tf_op jit(solution)/shard_map/ppermute | solution.py:47
  422.2 40.2 %copy-start.2 = (f32[196,384]{1,0:T(8,128)S(1)}, f32[196,384]{1,0:T(8,128)}, u32[]{:S(2)}) copy-start(f32[196,384]{1,0:T(8,128)} %pad_maximum_fusion.29) | copy-start | bytes 903172
  422.2 40.2 %copy-start.186 = (f32[384]{0:T(512)S(1)}, f32[384]{0:T(512)}, u32[]{:S(2)}) copy-start(f32[384]{0:T(512)} %get-tuple-element.1905) | copy-start | bytes 4612
  422.2 40.2 %copy-start.187 = (f32[384]{0:T(512)S(1)}, f32[384]{0:T(512)}, u32[]{:S(2)}) copy-start(f32[384]{0:T(512)} %get-tuple-element.1913) | copy-start | bytes 4612
  422.2 40.2 %copy-start.190 = (f32[384]{0:T(512)S(1)}, f32[384]{0:T(512)}, u32[]{:S(2)}) copy-start(f32[384]{0:T(512)} %get-tuple-element.1908) | copy-start | bytes 4612
  422.2 40.2 %copy-start.191 = (f32[384]{0:T(512)S(1)}, f32[384]{0:T(512)}, u32[]{:S(2)}) copy-start(f32[384]{0:T(512)} %get-tuple-element.1914) | copy-start | bytes 4612
  422.2 40.2 %copy-start.195 = (f32[384]{0:T(512)S(1)}, f32[384]{0:T(512)}, u32[]{:S(2)}) copy-start(f32[384]{0:T(512)} %get-tuple-element.1907) | copy-start | bytes 4612
  458.7 14.8 collective-permute-start
  520.4 132.2 %collective-permute-start.3 = (bf16[1,128,768]{2,1,0:T(8,128)(2,1)S(1)}, bf16[1,128,768]{2,1,0:T(8,128)(2,1)}, u32[]{:S(2)}, u32[]{:S(2)}) collective-permute-start(bf16[1,128,768]{2,1,0:T(8,128)(2,1)S(1)} %copy-done.185), channel_id=1, source_target_pairs={{16,0},{17,1},{18,2},{19,3},{20,4},{21,5},{22,6},{23,7},{24,8},{25... | collective-permute-start | bytes 589832 | tf_op jit(solution)/shard_map/ppermute | solution.py:47
  521.8 208.8 %collective-permute-start.2 = (bf16[1,128,768]{2,1,0:T(8,128)(2,1)}, bf16[1,128,768]{2,1,0:T(8,128)(2,1)}, u32[]{:S(2)}, u32[]{:S(2)}) collective-permute-start(bf16[1,128,768]{2,1,0:T(8,128)(2,1)} %get-tuple-element.602), channel_id=1, source_target_pairs={{16,0},{17,1},{18,2},{19,3},{20,4},{21,5},{22,6},{23,7},{24,8},{25... | collective-permute-start | bytes 589832 | tf_op jit(solution)/shard_map/ppermute | solution.py:47
  534.2 118.4 %copy-start.118 = (bf16[1,128,768]{2,1,0:T(8,128)(2,1)S(1)}, bf16[1,128,768]{2,1,0:T(8,128)(2,1)}, u32[]{:S(2)}) copy-start(bf16[1,128,768]{2,1,0:T(8,128)(2,1)} %bitcast_select_fusion.16) | copy-start | bytes 589828
  534.2 118.4 %copy-start.168 = (f32[768]{0:T(1024)S(1)}, f32[768]{0:T(1024)}, u32[]{:S(2)}) copy-start(f32[768]{0:T(1024)} %copy-done.167) | copy-start | bytes 9220
  534.2 118.4 %copy-start.193 = (f32[768]{0:T(1024)S(1)}, f32[768]{0:T(1024)}, u32[]{:S(2)}) copy-start(f32[768]{0:T(1024)} %copy-done.192) | copy-start | bytes 9220
  534.2 118.4 %copy-start.207 = (pred[2,128]{1,0:T(4,128)(4,1)S(1)}, pred[2,128]{1,0:T(4,128)(4,1)}, u32[]{:S(2)}) copy-start(pred[2,128]{1,0:T(4,128)(4,1)} %copy-done.206) | copy-start | bytes 772
  534.2 118.4 %copy-start.214 = (s32[2,128]{1,0:T(2,128)S(1)}, s32[2,128]{1,0:T(2,128)}, u32[]{:S(2)}) copy-start(s32[2,128]{1,0:T(2,128)} %param.46) | copy-start | bytes 3076
  534.2 118.4 %copy-start.217 = (f32[1,3072]{1,0:T(1,128)S(1)}, f32[1,3072]{1,0:T(1,128)}, u32[]{:S(2)}) copy-start(f32[1,3072]{1,0:T(1,128)} %constant_dynamic-slice_fusion.4) | copy-start | bytes 36868
  652.7 77.9 %copy-start.114 = (bf16[1,128,768]{2,1,0:T(8,128)(2,1)S(1)}, bf16[1,128,768]{2,1,0:T(8,128)(2,1)}, u32[]{:S(2)}) copy-start(bf16[1,128,768]{2,1,0:T(8,128)(2,1)} %copy-done.113) | copy-start | bytes 589828
  672.7 8.0 slice-start.4
  674.4 13.8 copy-start.19
  730.5 8.4 copy-start.11
  730.6 9.4 copy-start.43
  730.6 10.1 copy-start.44
  730.6 10.1 copy-start.178
  751.5 7.1 slice-start.6
  798.4 12.8 copy-start.180
  821.2 9.2 copy-start.45
  921.1 16.6 slice-start.8
  921.1 16.6 slice-start.9
  929.6 8.1 slice-start.10
  937.7 13.3 slice-start.13
  937.7 13.3 slice-start.14
  942.6 8.4 slice-start.15
  1517.6 7.8 copy-start.175
  1517.6 7.8 copy-start.177
  1517.7 7.8 copy-start.179
  1517.7 7.8 copy-start.181
  1517.7 168.8 %all-to-all-start = ((f32[16,5,9216]{2,1,0:T(8,128)}), f32[16,5,9216]{2,1,0:T(8,128)}, u32[]{:S(2)}, u32[]{:S(2)}) async-start(f32[16,5,9216]{2,1,0:T(8,128)} %all_to_all.10), calls=%async_computation.1 | async-start | bytes 9437184 | tf_op jit(solution)/shard_map/all_to_all | solution.py:526
  1523.6 160.7 %all-reduce.17.cloned.1.call-start = ((), (), s32[]{:S(2)}) async-start(), calls=%async_computation.4 | async-start | bytes 147456 | tf_op jit(solution)/shard_map/psum | solution.py:529
  1744.0 9.2 copy-start.3
  1753.2 8.2 copy-start.13
  1753.2 8.2 copy-start.7
  1753.2 8.2 copy-start.24
  2739.9 22.1 copy-start.53
  2739.9 9.6 copy-start.170
  2739.9 9.6 copy-start.171
  2739.9 9.6 copy-start.188
  2740.0 9.6 copy-start.189
  2740.0 11.8 copy-start.93
  2750.3 56.8 %collective-permute-start.5 = (bf16[18432]{0:T(1024)(128)(2,1)S(1)}, bf16[18432]{0:T(1024)(128)(2,1)S(1)}, u32[]{:S(2)}, u32[]{:S(2)}) collective-permute-start(bf16[18432]{0:T(1024)(128)(2,1)S(1)} %get-tuple-element.1973), channel_id=1, source_target_pairs={{0,16},{1,17},{2,18},{3,19},{4,20},{5,21},{6,22},{7,23},{8,24},{9,... | collective-permute-start | bytes 110600 | tf_op jit(solution)/shard_map/ppermute | solution.py:47
  2753.7 39.1 %copy-start.54 = (f32[5,128,384]{1,2,0:T(8,128)}, f32[5,128,384]{1,2,0:T(8,128)S(1)}, u32[]{:S(2)}) copy-start(f32[5,128,384]{1,2,0:T(8,128)S(1)} %fusion.721) | copy-start | bytes 2949124
  2762.1 13.0 copy-start.14
  2775.1 8.2 copy-start.12
  2783.3 9.6 copy-start.50
  2783.3 9.6 copy-start.51
  2791.3 16.5 collective-permute-start.4
  (98 other events, 293.2 us)
Sparse Core Ops, SparseCore 0:
  11.4 257.4 all-gather.1
  1021.1 487.1 reduce-scatter.1
  1530.5 153.8 all-reduce.16
where the time goes:
time: 2850 us; the launch traced here: 2840 us
  other arithmetic  1030 us (36%)
  waiting for transfers between devices  1010 us (35%)
  local copies, waits for them, and re-layouts  413 us (14%)
  matrix products  285 us (10%)
  blocking collectives  40.2 us (1%)
    another operation x23, other arithmetic, orthonormal(): factor = jnp.linalg.cholesky(mul(matrix.T, matrix))  553 us
    reduce_scatter x1, waiting for transfers between devices, on_device(): lax.psum_scatter(section_rows, 'dp', scatter_dimension=1, tiled=True)  487 us
    another operation x5, other arithmetic, orthonormal(): return jax.scipy.linalg.solve_triangular(factor, matrix.T, lower=True).T  301 us
    all_gather x1, waiting for transfers between devices, on_device(): lax.all_gather(weights[0].astype(jnp.bfloat16), 'dp', axis=0, tiled=True)  246 us
    psum x1, waiting for transfers between devices, on_device(): vec_total = lax.psum(vec_grads, 'dp')  157 us
    ppermute x6, waiting for transfers between devices, from_behind(): return lax.ppermute(shard, axis, pairs)  117 us
    unnamed x206, local copies, waits for them, and re-layouts  115 us
    dot_general x14, matrix products, mul(): return jnp.dot(left_op, right_op, precision=TOP_PRECISION)  108 us
  transfers between devices with their start and end apart: 10, of which 4 were waited for; matrix products, arithmetic and copies ran while one was open for 7% of the time, Pallas kernels for 0%

commit v1 on v0

--- a/solution.py
+++ b/solution.py
@@ -3,6 +3,8 @@
 import jax
 import jax.numpy as jnp
 from jax import lax
+from jax.experimental import pallas as pl
+from jax.experimental.pallas import tpu as pltpu
 from jax.sharding import PartitionSpec as P
 
 D = 768
@@ -15,9 +17,7 @@
 GRID = 14
 NT = 4
 LC = 128
-MB = 2
 STEP = 10
-IMG = 1
 P_SIZE = 196
 LT = 36
 NBE = 52
@@ -27,7 +27,6 @@
 VW = 18432
 
 
-TOP_PRECISION = lax.Precision.HIGHEST
 NORM_EPS = 1e-06
 ADAM_EPS = 1e-08
 BETA_FIRST = 0.5
@@ -39,6 +38,10 @@
 EMA_KEEP = 0.996
 CLIP_LIMIT = 1.0
 NEG_FILL = -1000000000.0
+WIRE = jnp.float16
+WIRE_TOP = 16384.0
+f32 = jnp.float32
+bf = jnp.bfloat16
 
 
 def from_behind(shard, axis, by):
@@ -61,33 +64,6 @@
 
 def pred_lengths():
     return [PD] * 8 + [PFF, PD, PD, PD, D, PD]
-
-
-def assemble(blocks, height, breadth):
-    block_edge = blocks.shape[-1]
-    tiled = blocks.reshape(height // block_edge, breadth // block_edge, block_edge, block_edge)
-    return tiled.transpose(0, 2, 1, 3).reshape(height, breadth)
-
-
-def split_blocks(matrix, block_edge):
-    height, breadth = matrix.shape
-    tiled = matrix.reshape(height // block_edge, block_edge, breadth // block_edge, block_edge)
-    return tiled.transpose(0, 2, 1, 3).reshape(-1, block_edge, block_edge)
-
-
-def unpack_mats(blocks, shapes):
-    block_edge = blocks.shape[-1]
-    result = []
-    offset = 0
-    for height, breadth in shapes:
-        amount = height * breadth // (block_edge * block_edge)
-        result.append(assemble(blocks[offset : offset + amount], height, breadth))
-        offset += amount
-    return result
-
-
-def pack_mats(matrices, block_edge):
-    return jnp.concatenate([split_blocks(matrix, block_edge) for matrix in matrices], 0)
 
 
 def unpack_vec(vector, lengths):
@@ -333,35 +309,366 @@
     return (grad_context, mats_out, vecs_out)
 
 
-def mul(left_op, right_op):
-    return jnp.dot(left_op, right_op, precision=TOP_PRECISION)
-
-
-def orthonormal(matrix):
-    factor = jnp.linalg.cholesky(mul(matrix.T, matrix))
-    return jax.scipy.linalg.solve_triangular(factor, matrix.T, lower=True).T
-
-
-def soap_update(weight, gradient, moment, second, left_op, right_op, left_stat, right_stat):
-    correct_one = 1.0 - BETA_FIRST**STEP
-    correct_two = 1.0 - BETA_SECOND**STEP
-    rotated = mul(mul(left_op.T, gradient), right_op)
-    moment_new = BETA_FIRST * moment + (1.0 - BETA_FIRST) * rotated
-    second_new = BETA_SECOND * second + (1.0 - BETA_SECOND) * rotated * rotated
-    normed = moment_new / correct_one / (jnp.sqrt(second_new / correct_two) + ADAM_EPS)
-    weight_new = weight - RATE_MATRIX * (
-        mul(mul(left_op, normed), right_op.T) + DECAY_MATRIX * weight
-    )
-    left_stat_new = BETA_STATS * left_stat + (1.0 - BETA_STATS) * mul(gradient, gradient.T)
-    right_stat_new = BETA_STATS * right_stat + (1.0 - BETA_STATS) * mul(gradient.T, gradient)
-    left_new = orthonormal(mul(left_stat_new, left_op))
-    right_new = orthonormal(mul(right_stat_new, right_op))
-    moment_out = mul(mul(mul(left_new.T, left_op), moment_new), mul(right_op.T, right_new))
-    return (weight_new, moment_out, second_new, left_new, right_new, left_stat_new, right_stat_new)
-
-
-def zero_mats(shapes):
-    return [jnp.zeros(shape, jnp.float32) for shape in shapes]
+DIMS = {"nn": (1, 0), "nt": (1, 1), "tn": (0, 0)}
+
+def parts_of(a, count):
+    found = []
+    for index in range(count):
+        piece = a.astype(bf)
+        found.append(piece)
+        if index + 1 < count:
+            a = a - piece.astype(f32)
+    return found
+
+def product(left, right, form, pairs):
+    ld, rd = DIMS[form]
+    lhs = jnp.concatenate([left[i] for i, _ in pairs], ld)
+    rhs = jnp.concatenate([right[j] for _, j in pairs], rd)
+    return lax.dot_general(lhs, rhs, (((ld,), (rd,)), ((), ())), preferred_element_type=f32)
+
+THREE = ((0, 1), (1, 0), (0, 0))
+SIX = ((0, 2), (2, 0), (1, 1), (0, 1), (1, 0), (0, 0))
+def mul3(left, right, form="nn"):
+    return product(left, right, form, THREE)
+def mul6(left, right, form="nn"):
+    return product(left, right, form, SIX)
+
+def invert_factors(mats):
+    n = mats[0].shape[0]
+    lane = lax.broadcasted_iota(jnp.int32, (8, n), 1)
+    sub = lax.broadcasted_iota(jnp.int32, (8, n), 0)
+    groups = [[a[8 * t : 8 * t + 8, :] for t in range(n // 8)] for a in mats]
+    for j in range(n):
+        top, at_row = divmod(j, 8)
+        here = lane == j
+        pick = jnp.full((8, n), j, jnp.int32)
+        for tiles in groups:
+            column = jnp.take_along_axis(tiles[top], pick, axis=1)
+            pivot = jnp.broadcast_to(column[at_row : at_row + 1, :], (8, n))
+            row = jnp.broadcast_to(tiles[top][at_row : at_row + 1, :], (8, n))
+            scaled = jnp.where(here, 1.0, row) * (1.0 / pivot)
+            for t in range(top, n // 8):
+                if t > top:
+                    column = jnp.take_along_axis(tiles[t], pick, axis=1)
+                fresh = jnp.where(here, 0.0, tiles[t]) - column * scaled
+                tiles[t] = jnp.where(sub > at_row, fresh, tiles[t]) if t == top else fresh
+    results = []
+    for tiles in groups:
+        rows = []
+        for t in range(n // 8):
+            at = sub + 8 * t
+            pivots = jnp.sum(jnp.where(lane == at, tiles[t], 0.0), axis=1, keepdims=True)
+            unit = jnp.where(lane < at, tiles[t], jnp.where(lane == at, 1.0, 0.0))
+            rows.append(unit * lax.rsqrt(pivots))
+        results.append(jnp.concatenate(rows, 0))
+    return results
+
+def first_kernel(flag, factor, g_ref, w_ref, m_ref, v_ref, l_ref, r_ref, e_ref, f_ref,
+                 w_out, m_out, v_out, e_out, f_out, base_out, gram_out):
+    on = flag[pl.program_id(0)] != 0
+
+    @pl.when(jnp.logical_not(on))
+    def keep():
+        for source, target in ((w_ref, w_out), (m_ref, m_out), (v_ref, v_out), (e_ref, e_out), (f_ref, f_out)):
+            target[...] = source[...]
+
+    @pl.when(on)
+    def update():
+        correct_one = 1.0 - BETA_FIRST**STEP
+        correct_two = 1.0 - BETA_SECOND**STEP
+        grad = parts_of(g_ref[0] * factor[0], 3)
+        left = parts_of(l_ref[0], 3)
+        right = parts_of(r_ref[0], 3)
+        rotated = mul3(left, parts_of(mul3(grad, right), 2), "tn")
+        moment = BETA_FIRST * m_ref[0] + (1.0 - BETA_FIRST) * rotated
+        second = BETA_SECOND * v_ref[0] + (1.0 - BETA_SECOND) * rotated * rotated
+        m_out[0] = moment
+        v_out[0] = second
+        normed = moment / correct_one / (jnp.sqrt(second / correct_two) + ADAM_EPS)
+        weight = w_ref[0]
+        step = mul3(left, parts_of(mul3(parts_of(normed, 2), right, "nt"), 2))
+        w_out[0] = weight - RATE_MATRIX * (step + DECAY_MATRIX * weight)
+        for index, (stat, target, basis, form) in enumerate(
+            ((e_ref, e_out, left, "nt"), (f_ref, f_out, right, "tn"))
+        ):
+            fresh = BETA_STATS * stat[0] + (1.0 - BETA_STATS) * mul6(grad, grad, form)
+            target[0] = fresh
+            moved = mul6(parts_of(fresh, 3), basis)
+            base_out[0, index] = moved
+            pieces = parts_of(moved, 3)
+            gram_out[0, index] = mul6(pieces, pieces, "tn")
+
+def factor_kernel(flag, base_ref, gram_ref, q_out, base, gram, inverse):
+    blocks, edge = base_ref.shape[0], base_ref.shape[-1]
+    panel = 128
+    count = edge // panel
+    base[...] = base_ref[...]
+    gram[...] = gram_ref[...]
+
+    def stage(k):
+        at = pl.ds(panel * k, panel)
+        start = panel * k
+        spot = slice(start, start + panel)
+        rest = slice(start + panel, edge)
+
+        def block(b, carry):
+            @pl.when(flag[b] != 0)
+            def run():
+                for side in range(2):
+                    inv = parts_of(inverse[b, side], 3)
+                    q = mul6(parts_of(base[b, side, :, spot], 3), inv, "nt")
+                    q_out[b, side, :, spot] = q
+                    if k + 1 < count:
+                        p = parts_of(mul6(inv, parts_of(gram[b, side, spot, rest], 3)), 3)
+                        gram[b, side, rest, rest] = gram[b, side, rest, rest] - mul6(p, p, "tn")
+                        base[b, side, :, rest] = base[b, side, :, rest] - mul6(parts_of(q, 3), p)
+            return carry
+
+        lax.fori_loop(0, blocks, block, 0)
+
+    def turn(k, carry):
+        for which in range(count):
+            @pl.when(k == which)
+            def load():
+                spot = slice(panel * which, panel * which + panel)
+                for b in range(blocks):
+                    for side in range(2):
+                        inverse[b, side] = gram[b, side, spot, spot]
+        mats = invert_factors([inverse[b, side] for b in range(blocks) for side in range(2)])
+        for b in range(blocks):
+            for side in range(2):
+                inverse[b, side] = mats[2 * b + side]
+        for which in range(count):
+            @pl.when(k == which)
+            def run():
+                stage(which)
+        return carry
+
+    lax.fori_loop(0, count, turn, 0)
+
+def last_kernel(flag, l_ref, r_ref, m_ref, q_ref, l_out, r_out, m_out):
+    on = flag[pl.program_id(0)] != 0
+
+    @pl.when(jnp.logical_not(on))
+    def keep():
+        l_out[...] = l_ref[...]
+        r_out[...] = r_ref[...]
+        m_out[...] = m_ref[...]
+
+    @pl.when(on)
+    def update():
+        l_out[0] = q_ref[0, 0]
+        r_out[0] = q_ref[0, 1]
+        turn_left = mul3(parts_of(q_ref[0, 0], 2), parts_of(l_ref[0], 2), "tn")
+        turn_right = mul3(parts_of(r_ref[0], 2), parts_of(q_ref[0, 1], 2), "tn")
+        half = mul3(parts_of(turn_left, 2), parts_of(m_ref[0], 2))
+        m_out[0] = mul3(parts_of(half, 2), parts_of(turn_right, 2))
+
+def soap_first(flags, factor, *arrays):
+    n, e = arrays[0].shape[:2]
+    one = pl.BlockSpec((1, e, e), lambda i, *_: (i, 0, 0))
+    two = pl.BlockSpec((1, 2, e, e), lambda i, *_: (i, 0, 0, 0))
+    single = jax.ShapeDtypeStruct((n, e, e), f32)
+    double = jax.ShapeDtypeStruct((n, 2, e, e), f32)
+    return pl.pallas_call(
+        first_kernel,
+        grid_spec=pltpu.PrefetchScalarGridSpec(
+            num_scalar_prefetch=2, grid=(n,), in_specs=[one] * 8, out_specs=[one] * 5 + [two] * 2
+        ),
+        out_shape=[single] * 5 + [double] * 2,
+        compiler_params=pltpu.CompilerParams(vmem_limit_bytes=56 << 20),
+        name="soap_first",
+    )(flags, factor, *arrays)
+
+
+def soap_factor(flags, base, gram):
+    n, _, e, _ = base.shape
+    whole = pl.BlockSpec(memory_space=pltpu.VMEM)
+    return pl.pallas_call(
+        factor_kernel,
+        grid_spec=pltpu.PrefetchScalarGridSpec(
+            num_scalar_prefetch=1,
+            grid=(),
+            in_specs=[whole] * 2,
+            out_specs=whole,
+            scratch_shapes=[
+                pltpu.VMEM((n, 2, e, e), f32),
+                pltpu.VMEM((n, 2, e, e), f32),
+                pltpu.VMEM((n, 2, 128, 128), f32),
+            ],
+        ),
+        out_shape=jax.ShapeDtypeStruct(base.shape, f32),
+        compiler_params=pltpu.CompilerParams(vmem_limit_bytes=56 << 20),
+        name="soap_factor",
+    )(flags, base, gram)
+
+
+def soap_last(flags, left, right, moment, fresh):
+    n, e = left.shape[:2]
+    one = pl.BlockSpec((1, e, e), lambda i, *_: (i, 0, 0))
+    two = pl.BlockSpec((1, 2, e, e), lambda i, *_: (i, 0, 0, 0))
+    return pl.pallas_call(
+        last_kernel,
+        grid_spec=pltpu.PrefetchScalarGridSpec(
+            num_scalar_prefetch=1, grid=(n,), in_specs=[one] * 3 + [two], out_specs=[one] * 3
+        ),
+        out_shape=[jax.ShapeDtypeStruct((n, e, e), f32)] * 3,
+        compiler_params=pltpu.CompilerParams(vmem_limit_bytes=56 << 20),
+        name="soap_last",
+    )(flags, left, right, moment, fresh)
+
+
+def block_places(shapes, edge):
+    places = []
+    for index, (height, breadth) in enumerate(shapes):
+        for row in range(height // edge):
+            for column in range(breadth // edge):
+                places.append((index, row, column))
+    return places
+
+
+def gather_matrices(slots, second, table):
+    edge = table.shape[-1]
+    shapes = enc_shapes() + pred_shapes()
+    places = block_places(shapes, edge)
+
+    def body(slots_ref, second_ref, table_ref, *rest):
+        outs, sems = rest[:-1], rest[-1]
+
+        def copy(j):
+            index, row, column = places[j]
+            spot = outs[index].at[pl.ds(row * edge, edge), pl.ds(column * edge, edge)]
+            return pltpu.make_async_copy(table_ref.at[slots_ref[j]], spot, sems.at[j])
+
+        for j in range(NBE):
+            copy(j).start()
+
+        @pl.when(second_ref[0] != 0)
+        def more():
+            for j in range(NBE, NBE + NBP):
+                copy(j).start()
+            for j in range(NBE, NBE + NBP):
+                copy(j).wait()
+
+        for j in range(NBE):
+            copy(j).wait()
+
+    result = pl.pallas_call(
+        body,
+        grid_spec=pltpu.PrefetchScalarGridSpec(
+            num_scalar_prefetch=2,
+            grid=(),
+            in_specs=[pl.BlockSpec(memory_space=pl.ANY)],
+            out_specs=[pl.BlockSpec(memory_space=pltpu.VMEM)] * len(shapes),
+            scratch_shapes=[pltpu.SemaphoreType.DMA((len(places),))],
+        ),
+        out_shape=[jax.ShapeDtypeStruct(shape, table.dtype) for shape in shapes],
+        compiler_params=pltpu.CompilerParams(vmem_limit_bytes=56 << 20),
+        name="gather_matrices",
+    )(slots, second, table)
+    return result[: len(enc_shapes())], result[len(enc_shapes()) :]
+
+
+def place_shares(slots, second, enc_share, pred_share, slot_rows):
+    depth, edge = enc_share.shape[1:]
+
+    def body(slots_ref, second_ref, enc_ref, pred_ref, out_ref):
+        def run(source, first, count):
+            def copy(j, carry):
+                out_ref[slots_ref[first + j]] = source[j]
+                return carry
+
+            lax.fori_loop(0, count, copy, 0)
+
+        @pl.when(second_ref[0] == 0)
+        def enc():
+            run(enc_ref, 0, NBE)
+
+        @pl.when(second_ref[0] != 0)
+        def pred():
+            run(pred_ref, NBE, NBP)
+
+    return pl.pallas_call(
+        body,
+        grid_spec=pltpu.PrefetchScalarGridSpec(
+            num_scalar_prefetch=2,
+            grid=(),
+            in_specs=[pl.BlockSpec(memory_space=pltpu.VMEM)] * 2,
+            out_specs=pl.BlockSpec(memory_space=pltpu.VMEM),
+        ),
+        out_shape=jax.ShapeDtypeStruct((slot_rows, depth, edge), f32),
+        compiler_params=pltpu.CompilerParams(vmem_limit_bytes=40 << 20),
+        name="place_shares",
+    )(slots, second, enc_share, pred_share)
+
+
+class Exchange:
+    def __init__(self, sections):
+        self.ranks = lax.axis_size("dp")
+        self.bits = self.ranks.bit_length() - 1
+        self.sections = sections
+
+    def swap(self, value, bit):
+        pairs = [
+            (s * self.ranks + i, s * self.ranks + (i ^ (1 << bit)))
+            for s in self.sections
+            for i in range(self.ranks)
+        ]
+        return lax.ppermute(value, ("section", "dp"), pairs)
+
+    def total(self, value):
+        for bit in range(self.bits):
+            value = value + self.swap(value, bit)
+        return value
+
+
+def power_scale(bound):
+    return jnp.exp2(jnp.floor(jnp.log2(WIRE_TOP / jnp.maximum(bound, 1e-30))))
+
+
+def halve(exchange, grads, orders):
+    ranks, bits = exchange.ranks, exchange.bits
+    me = lax.axis_index("dp")
+    bounds = [jnp.max(jnp.abs(g)) for g in grads]
+    parts = []
+    for g in grads:
+        lead, edge, columns = g.shape
+        parts.append(g.reshape((lead,) + (2,) * bits + (edge // ranks, columns)))
+    left = [list(range(bits - 1, -1, -1)) for _ in grads]
+    for stage in range(bits):
+        sent, tiny = [], {}
+        for k, part in enumerate(parts):
+            bit = orders[k][stage]
+            axis = 1 + left[k].index(bit)
+            mine = (me >> bit) & 1
+            give = lax.dynamic_index_in_dim(part, 1 - mine, axis, keepdims=False)
+            keep = lax.dynamic_index_in_dim(part, mine, axis, keepdims=False)
+            scale = power_scale(bounds[k])
+            low = (give.reshape(-1, give.shape[-1]) * scale).astype(WIRE)
+            sent.append((exchange.swap(low, bit), keep))
+            tiny.setdefault(bit, []).append(k)
+            left[k].remove(bit)
+        for bit, members in tiny.items():
+            packed = jnp.stack([bounds[k] for k in members])
+            packed = jnp.pad(packed, (0, 128 - len(members)))
+            theirs = exchange.swap(packed, bit)
+            for place, k in enumerate(members):
+                other = theirs[place]
+                low, keep = sent[k]
+                got = low.astype(f32) * (1.0 / power_scale(other))
+                parts[k] = keep + got.reshape(keep.shape)
+                bounds[k] = bounds[k] + other
+    return parts
+
+
+def split_columns(share, edge):
+    lead, depth, columns = share.shape
+    cut = share.reshape(lead, depth, columns // edge, edge)
+    return cut.transpose(0, 2, 1, 3).reshape(-1, depth, edge)
+
+
+def zeros_of(shapes):
+    return jax.tree.map(lambda leaf: jnp.zeros(leaf.shape, leaf.dtype), shapes)
 
 
 def on_device(
@@ -384,15 +691,16 @@
 ):
     section_index = lax.axis_index("section")
     owner_index = lax.axis_index("dp")
+    ranks = lax.axis_size("dp")
     is_first = section_index == 0
+    second = section_index.astype(jnp.int32).reshape(1)
     slot_count = weights.shape[1]
-    block_edge = weights.shape[-1]
-    slot_rows = slot_count * lax.axis_size("dp")
-    gathered = lax.all_gather(weights[0].astype(jnp.bfloat16), "dp", axis=0, tiled=True)
+    edge = weights.shape[-1]
+    slot_rows = slot_count * ranks
+    gathered = lax.all_gather(weights[0].astype(bf), "dp", axis=0, tiled=True)
+    enc_mats, pred_mats = gather_matrices(slot_of, second, gathered)
     enc_slots = slot_of[:NBE]
     pred_slots = slot_of[NBE:]
-    enc_mats = unpack_mats(jnp.take(gathered, enc_slots, 0), enc_shapes())
-    pred_mats = unpack_mats(jnp.take(gathered, pred_slots, 0), pred_shapes())
     row_now = vectors[0]
     enc_vectors = unpack_vec(
         lax.dynamic_slice_in_dim(row_now, section_index * VP, VE), enc_lengths()
@@ -400,133 +708,141 @@
     pred_vectors = unpack_vec(row_now[:VP], pred_lengths())
     pos_enc = sincos(D)
     pos_pred = sincos(PD)
-    local_images = ctx_idx.shape[0]
+    images = ctx_idx.shape[0]
     ctx_valid = jnp.arange(LC)[None, :] < ctx_len[:, None]
-    tgt_flat = tgt_idx.reshape(local_images, NT * LT)
-    tgt_valid = (jnp.arange(LT)[None, None, :] < tgt_len[:, :, None]).reshape(local_images, NT * LT)
-    contexts = []
-    targets = []
-    for micro_index in range(MB):
-        window = slice(micro_index * IMG, (micro_index + 1) * IMG)
-        pixel_rows = jnp.take_along_axis(pixels[window], ctx_idx[window][:, :, None], 1)
-
-        def run_encoder(unused):
-            encoded, _ = encode_forward(
-                pixel_rows,
-                jnp.take(pos_enc, ctx_idx[window], 0),
-                ctx_valid[window],
-                enc_mats,
-                enc_vectors,
-            )
-            return encoded.astype(jnp.bfloat16)
-
-        def skip_encoder(unused):
-            return jnp.zeros((IMG, LC, D), jnp.bfloat16)
-
-        outgoing = lax.cond(is_first, run_encoder, skip_encoder, 0)
-        contexts.append(from_behind(outgoing, "section", 1))
-
-        def run_target(unused):
-            return target_forward(
-                pixels[window], tgt_flat[window], pos_enc[None], enc_mats, enc_vectors
-            )
-
-        def skip_target(unused):
-            return jnp.zeros((IMG, NT * LT, D), jnp.float32)
-
-        targets.append(lax.cond(is_first, skip_target, run_target, 0))
-    enc_acc = zero_mats(enc_shapes())
-    pred_acc = zero_mats(pred_shapes())
-    vec_grads = jnp.zeros((VW,), jnp.float32)
-    loss_local = jnp.zeros((), jnp.float32)
-    for micro_index in reversed(range(MB)):
-        window = slice(micro_index * IMG, (micro_index + 1) * IMG)
-        pixel_rows = jnp.take_along_axis(pixels[window], ctx_idx[window][:, :, None], 1)
-        joined_valid = jnp.concatenate([ctx_valid[window], tgt_valid[window]], 1)
-        target_mask = tgt_valid[window].astype(jnp.float32)[:, :, None]
-
-        def run_predictor(unused):
-            context = contexts[micro_index]
-            predicted, kept = predict_forward(
-                context,
-                jnp.take(pos_pred, ctx_idx[window], 0),
-                jnp.take(pos_pred, tgt_flat[window], 0),
-                joined_valid,
-                pred_mats,
-                pred_vectors,
-            )
-            difference = predicted - targets[micro_index]
-            magnitude = jnp.abs(difference)
-            loss_value = jnp.sum(
-                jnp.where(magnitude < 1.0, 0.5 * difference * difference, magnitude - 0.5)
-                * target_mask
-            )
-            grad_out = jnp.clip(difference, -1.0, 1.0) * target_mask
-            grad_context, mats_grad, vecs_grad = predict_backward(
-                context, kept, grad_out, pred_mats, pred_vectors
-            )
-            return (
-                grad_context.astype(jnp.bfloat16),
-                mats_grad,
-                jnp.concatenate(vecs_grad),
-                loss_value,
-            )
-
-        def skip_predictor(unused):
-            return (
-                jnp.zeros((IMG, LC, D), jnp.bfloat16),
-                zero_mats(pred_shapes()),
-                jnp.zeros((VP,), jnp.float32),
-                jnp.zeros((), jnp.float32),
-            )
-
-        back_send, pred_part, pred_vec_part, loss_part = lax.cond(
-            is_first, skip_predictor, run_predictor, 0
+    tgt_flat = tgt_idx.reshape(images, NT * LT)
+    tgt_valid = (jnp.arange(LT)[None, None, :] < tgt_len[:, :, None]).reshape(images, NT * LT)
+
+    def pick(index, count):
+        return (index[..., None] == jnp.arange(count)).astype(f32)
+
+    ctx_hot = pick(ctx_idx, P_SIZE)
+    tgt_hot = pick(tgt_flat, P_SIZE)
+
+    def choose(hot, table):
+        return jnp.einsum(
+            "njp,pd->njd", hot, table, precision=lax.Precision.HIGHEST, preferred_element_type=f32
         )
-        incoming = from_behind(back_send, "section", -1)
-
-        def run_encoder_back(unused):
-            encoded, kept = encode_forward(
-                pixel_rows,
-                jnp.take(pos_enc, ctx_idx[window], 0),
-                ctx_valid[window],
-                enc_mats,
-                enc_vectors,
-            )
-            mats_grad, vecs_grad = encode_backward(
-                pixel_rows, kept, incoming.astype(jnp.float32), enc_mats, enc_vectors
-            )
-            return (mats_grad, jnp.concatenate(vecs_grad))
-
-        def skip_encoder_back(unused):
-            return (zero_mats(enc_shapes()), jnp.zeros((VE,), jnp.float32))
-
-        enc_part, enc_vec_part = lax.cond(is_first, run_encoder_back, skip_encoder_back, 0)
-        vec_grads = (
-            vec_grads + jnp.pad(enc_vec_part, (0, VW - VE)) + jnp.pad(pred_vec_part, (0, VW - VP))
+
+    pixel_rows = jnp.einsum(
+        "njp,npd->njd", ctx_hot.astype(bf), pixels, preferred_element_type=f32
+    ).astype(bf)
+
+    def run_encoder(unused):
+        encoded, kept = encode_forward(
+            pixel_rows, choose(ctx_hot, pos_enc), ctx_valid, enc_mats, enc_vectors
         )
-        loss_local = loss_local + loss_part
-        enc_acc = [total + part for total, part in zip(enc_acc, enc_part)]
-        pred_acc = [total + part for total, part in zip(pred_acc, pred_part)]
-    count_local = jnp.where(is_first, 0, jnp.sum(tgt_len)).astype(jnp.float32)
-    loss_total, count_total = lax.psum((loss_local, count_local), ("section", "dp"))
-    enc_grads = pack_mats(enc_acc, block_edge)
-    pred_grads = pack_mats(pred_acc, block_edge)
-    entry_count = block_edge * block_edge
-    padded_pred = jnp.pad(pred_grads, ((0, NBE - NBP), (0, 0), (0, 0)))
-    section_rows = jnp.where(is_first, enc_grads, padded_pred).reshape(NBE, entry_count)
-    column_part = lax.psum_scatter(section_rows, "dp", scatter_dimension=1, tiled=True)
-    spare_slots = jnp.full((NBE - NBP,), slot_rows, jnp.int32)
-    destination = jnp.where(is_first, enc_slots, jnp.concatenate([pred_slots, spare_slots]))
-    placed = (
-        jnp.zeros((slot_rows, column_part.shape[1]), jnp.float32)
-        .at[destination]
-        .add(column_part, mode="drop")
-    )
-    owned_sum = lax.all_to_all(placed, "dp", split_axis=0, concat_axis=1, tiled=True).reshape(
-        slot_count, block_edge, block_edge
-    )
-    vec_total = lax.psum(vec_grads, "dp")
+        return encoded.astype(bf), kept
+
+    kept_shapes = jax.eval_shape(run_encoder, 0)[1]
+
+    def enc_branch(unused):
+        encoded, kept = run_encoder(0)
+        return encoded, kept, jnp.zeros((images, NT * LT, D), f32)
+
+    def tgt_branch(unused):
+        valid = jnp.ones(pixels.shape[:2], jnp.bool_)
+        encoded, _ = encode_forward(pixels, pos_enc[None], valid, enc_mats, enc_vectors)
+        target = jnp.einsum(
+            "njp,npd->njd",
+            tgt_hot,
+            plain_norm(encoded),
+            precision=lax.Precision.HIGHEST,
+            preferred_element_type=f32,
+        )
+        return jnp.zeros((images, LC, D), bf), zeros_of(kept_shapes), target
+
+    outgoing, kept, target = lax.cond(is_first, enc_branch, tgt_branch, 0)
+    context = from_behind(outgoing, "section", 1)
+    joined_valid = jnp.concatenate([ctx_valid, tgt_valid], 1)
+    target_mask = tgt_valid.astype(f32)[:, :, None]
+
+    def run_predictor(unused):
+        predicted, saved = predict_forward(
+            context,
+            choose(ctx_hot, pos_pred),
+            choose(tgt_hot, pos_pred),
+            joined_valid,
+            pred_mats,
+            pred_vectors,
+        )
+        difference = predicted - target
+        magnitude = jnp.abs(difference)
+        loss_value = jnp.sum(
+            jnp.where(magnitude < 1.0, 0.5 * difference * difference, magnitude - 0.5)
+            * target_mask
+        )
+        grad_out = jnp.clip(difference, -1.0, 1.0) * target_mask
+        grad_context, mats_grad, vecs_grad = predict_backward(
+            context, saved, grad_out, pred_mats, pred_vectors
+        )
+        return grad_context.astype(bf), mats_grad, jnp.concatenate(vecs_grad), loss_value
+
+    predictor_shapes = jax.eval_shape(run_predictor, 0)
+    back_send, pred_grads, pred_vec, loss_local = lax.cond(
+        is_first, lambda unused: zeros_of(predictor_shapes), run_predictor, 0
+    )
+    incoming = from_behind(back_send, "section", -1)
+
+    low_order = list(range(Exchange((0,)).bits))
+    swapped = [1, 0] + low_order[2:] if len(low_order) > 1 else low_order
+    g_in, g_qkv, g_out, g_up, g_down, g_last = pred_grads
+    pred_leaves = [
+        jnp.concatenate([g_qkv, g_out, g_up, g_last], 1)[None],
+        jnp.concatenate([g_in, g_down], 0).reshape(-1, edge, PD),
+    ]
+    pred_wide, pred_tall = halve(Exchange((1,)), pred_leaves, [low_order, swapped])
+
+    def run_encoder_back(unused):
+        mats_grad, vecs_grad = encode_backward(
+            pixel_rows, kept, incoming.astype(f32), enc_mats, enc_vectors
+        )
+        return mats_grad, jnp.concatenate(vecs_grad)
+
+    back_shapes = jax.eval_shape(run_encoder_back, 0)
+    enc_grads, enc_vec = lax.cond(
+        is_first, run_encoder_back, lambda unused: zeros_of(back_shapes), 0
+    )
+    enc_leaves = [g.reshape(-1, edge, g.shape[1]) for g in enc_grads]
+    e_patch, e_qkv, e_out, e_up, e_down = enc_leaves
+    s_up, s_down = halve(Exchange((0,)), [e_up, e_down], [low_order, swapped])
+    s_qkv, s_out, s_patch = halve(
+        Exchange((0,)), [e_qkv, e_out, e_patch], [low_order, swapped, swapped]
+    )
+    enc_share = jnp.concatenate(
+        [split_columns(s, edge) for s in (s_patch, s_qkv, s_out, s_up, s_down)], 0
+    )
+    wide = split_columns(pred_wide, edge)
+    pred_share = jnp.concatenate([pred_tall[:2], wide[:8], pred_tall[2:], wide[8:]], 0)
+
+    both = Exchange((0, 1))
+    vec_local = jnp.where(is_first, enc_vec, jnp.pad(pred_vec, (0, VE - VP)))
+    count_local = jnp.where(is_first, 0, jnp.sum(tgt_len)).astype(f32)
+    scalars = jnp.pad(jnp.stack([loss_local, count_local]), (0, 126))
+    summed = both.total(jnp.concatenate([vec_local, scalars]))
+    vec_total = jnp.pad(summed[:VE], (0, VW - VE))
+    share_squares = jnp.where(
+        is_first, jnp.sum(enc_share * enc_share), jnp.sum(pred_share * pred_share)
+    )
+    squares = both.total(jnp.full((128,), share_squares))
+    facts = jnp.stack([squares[0] + jnp.sum(summed[:VE] ** 2), summed[VE], summed[VE + 1]])
+    facts = jnp.pad(facts, (0, 125))
+    swap_sections = [(i, 1 - i) for i in range(2)]
+    facts = facts + lax.ppermute(facts, "section", swap_sections)
+    square_total, loss_total, count_total = facts[0], facts[1], facts[2]
+
+    placed = place_shares(slot_of, second, enc_share, pred_share, slot_rows)
+    bound = jnp.where(is_first, jnp.max(jnp.abs(enc_share)), jnp.max(jnp.abs(pred_share)))
+    exponent = jnp.floor(jnp.log2(WIRE_TOP / jnp.maximum(bound, 1e-30)))
+    depth = edge // ranks
+    payload = (placed * jnp.exp2(exponent)).reshape(ranks, slot_count * depth, edge)
+    mark = jnp.full((ranks, 8, edge), exponent)
+    payload = jnp.concatenate([payload, mark], 1).astype(WIRE)
+    owned = lax.all_to_all(payload, "dp", split_axis=0, concat_axis=0, tiled=True).astype(f32)
+    unscale = 1.0 / jnp.exp2(owned[:, -1:, :1])
+    owned = (owned[:, : slot_count * depth] * unscale).reshape(ranks, slot_count, depth, edge)
+    owned_sum = owned.transpose(1, 0, 2, 3).reshape(slot_count, edge, edge)
+
     own_ids = owner_index * slot_count + jnp.arange(slot_count)
     enc_here = jnp.any(own_ids[:, None] == enc_slots[None, :], 1)
     pred_here = jnp.any(own_ids[:, None] == pred_slots[None, :], 1)
@@ -535,15 +851,14 @@
     positions = jnp.arange(VW)
     vec_trained = positions < jnp.where(is_first, VE, VP)
     vec_ema = jnp.logical_and(jnp.logical_not(is_first), positions >= VP)
-    block_squares = jnp.sum(jnp.where(trained[:, None, None], owned_sum * owned_sum, 0.0))
-    vec_squares = jnp.where(
-        owner_index == 0, jnp.sum(jnp.where(vec_trained, vec_total * vec_total, 0.0)), 0.0
-    )
-    squares = block_squares + vec_squares
-    square_total = lax.psum(squares, ("section", "dp"))
     grad_norm = jnp.sqrt(square_total) / count_total
     factor = jnp.minimum(1.0, CLIP_LIMIT / (grad_norm + 1e-06)) / count_total
-    olds = (
+
+    flags = trained.astype(jnp.int32)
+    new_weight, moment, new_second, new_estat, new_fstat, base, gram = soap_first(
+        flags,
+        factor.reshape(1),
+        owned_sum,
         weights[0],
         first_moment[0],
         second_moment[0],
@@ -552,12 +867,11 @@
         left_stats[0],
         right_stats[0],
     )
-    results = jax.vmap(soap_update)(
-        olds[0], owned_sum * factor, olds[1], olds[2], olds[3], olds[4], olds[5], olds[6]
-    )
-    updated = [
-        jnp.where(trained[:, None, None], fresh, stale) for fresh, stale in zip(results, olds)
-    ]
+    fresh_bases = soap_factor(flags, base, gram)
+    new_left, new_right, new_first = soap_last(
+        flags, left_basis[0], right_basis[0], moment, fresh_bases
+    )
+
     correct_one = 1.0 - BETA_FIRST**STEP
     correct_two = 1.0 - BETA_SECOND**STEP
     vec_clipped = vec_total * factor
@@ -569,26 +883,24 @@
     new_vec = jnp.where(vec_trained, stepped, row_now)
     new_vec_first = jnp.where(vec_trained, fresh_first, vector_first[0])
     new_vec_second = jnp.where(vec_trained, fresh_second, vector_second[0])
-    from_encoder, vec_from_encoder = (
-        from_behind(updated[0].astype(jnp.bfloat16), "section", 1).astype(jnp.float32),
-        from_behind(new_vec.astype(jnp.bfloat16), "section", 1).astype(new_vec.dtype),
-    )
-    updated[0] = jnp.where(
-        ema_here[:, None, None], EMA_KEEP * weights[0] + (1.0 - EMA_KEEP) * from_encoder, updated[0]
-    )
-    aligned = jnp.concatenate([jnp.zeros((VP,), jnp.float32), vec_from_encoder[:VE]])
+    from_encoder = from_behind(new_weight.astype(bf), "section", 1).astype(f32)
+    vec_from_encoder = from_behind(new_vec.astype(bf), "section", 1).astype(f32)
+    new_weight = jnp.where(
+        ema_here[:, None, None], EMA_KEEP * weights[0] + (1.0 - EMA_KEEP) * from_encoder, new_weight
+    )
+    aligned = jnp.concatenate([jnp.zeros((VP,), f32), vec_from_encoder[:VE]])
     new_vec = jnp.where(vec_ema, EMA_KEEP * row_now + (1.0 - EMA_KEEP) * aligned, new_vec)
     return (
         loss_total,
         count_total,
         grad_norm,
-        updated[0][None],
-        updated[1][None],
-        updated[2][None],
-        updated[3][None],
-        updated[4][None],
-        updated[5][None],
-        updated[6][None],
+        new_weight[None],
+        new_first[None],
+        new_second[None],
+        new_left[None],
+        new_right[None],
+        new_estat[None],
+        new_fstat[None],
         new_vec[None],
         new_vec_first[None],
         new_vec_second[None],

time: 2850 us -> 1180 us (0.41)
  other arithmetic: 1030 us -> 116 us
  waiting for transfers between devices: 1010 us -> 472 us
  local copies, waits for them, and re-layouts: 413 us -> 116 us
  matrix products: 285 us -> 89 us
  starting transfers between devices: 15.9 us -> 157 us
  Pallas kernels: 0 us -> 135 us
  between operations: 21.9 us -> 62.6 us
  blocking collectives: 40.2 us -> 0 us
    another operation x28 -> x13, other arithmetic: 854 us -> 5.33 us  [the longest x8 3.46 us: halve(): packed = jnp.stack([bounds[k] for k in members])]
    reduce_scatter x1 -> x0, waiting for transfers between devices: 487 us -> none  [on_device(): lax.psum_scatter(section_rows, 'dp', scatter_dimension=1, tiled=True)]
    psum x1 -> x0, waiting for transfers between devices: 157 us -> none  [on_device(): vec_total = lax.psum(vec_grads, 'dp')]
    pallas_call x0 -> x5, Pallas kernels: none -> 135 us  [the longest x1 64.2 us: soap_factor(): pl.pallas_call(factor_kernel, grid_spec=pltpu.PrefetchScalarGridSpec(num_...]
    ppermute x0 -> x55, starting transfers between devices: none -> 124 us  [the longest x54 124 us: swap(): return lax.ppermute(value, ('section', 'dp'), pairs)]
    dot_general x16 -> x2, matrix products: 113 us -> 2.31 us  [the longest x1 1.99 us: choose(): jnp.einsum('njp,pd->njd', hot, table, precision=lax.Precision.HIGHEST, pr...]
    unnamed x206 -> x131, local copies, waits for them, and re-layouts: 115 us -> 10.2 us
    ppermute x0 -> x55, waiting for transfers between devices: none -> 95.5 us  [the longest x54 94.9 us: swap(): return lax.ppermute(value, ('section', 'dp'), pairs)]
  transfers between devices with their start and end apart: 10 -> 61, of which waited for: 4 -> 30; matrix products, arithmetic and copies ran while one was open for 7% -> 20% of each run, Pallas kernels for 0% -> 7%
where the time goes in v1:
time: 1180 us; the launch traced here: 1160 us
  waiting for transfers between devices  472 us (40%)
  starting transfers between devices  157 us (13%)
  Pallas kernels  135 us (11%)
  local copies, waits for them, and re-layouts  116 us (10%)
  other arithmetic  116 us (10%)
  matrix products  89 us (8%)
  between operations  62.6 us (5%)
  loops' own time  14.8 us (1%)
    all_gather x1, waiting for transfers between devices, on_device(): gathered = lax.all_gather(weights[0].astype(bf), 'dp', axis=0, tiled=True)  253 us
    ppermute x54, starting transfers between devices, swap(): return lax.ppermute(value, ('section', 'dp'), pairs)  124 us
    ppermute x4, waiting for transfers between devices, from_behind(): return lax.ppermute(shard, axis, pairs)  124 us
    ppermute x54, waiting for transfers between devices, swap(): return lax.ppermute(value, ('section', 'dp'), pairs)  94.9 us
    pallas_call x1, Pallas kernels, soap_factor(): pl.pallas_call(factor_kernel, grid_spec=pltpu.PrefetchScalarGridSpec(num_...  64.2 us
    pallas_call x1, Pallas kernels, soap_first(): pl.pallas_call(first_kernel, grid_spec=pltpu.PrefetchScalarGridSpec(num_s...  42.2 us
    cond x5, local copies, waits for them, and re-layouts, on_device(): lax.cond(is_first, run_encoder_back, lambda unused: zeros_of(back_shapes)...  33.3 us
    dot_general x4, matrix products, dense_back(): jnp.einsum('...m,km->...k', grad_low, weight, preferred_element_type=jnp....  32.6 us
  transfers between devices with their start and end apart: 61, of which 30 were waited for; matrix products, arithmetic and copies ran while one was open for 20% of the time, Pallas kernels for 7%

profile of v1, /device:TPU:4, one launch (start us, length us, event | category | flops | bytes accessed | tf_op | source)
XLA Modules:
  0.0 1162.6 jit_solution(4207057451875496587)
XLA Ops:
  7.3 3.1 bitcast_convert_fusion
  15.8 253.2 %all-gather.2.cloned.1.call-done.table_ref = bf16[80,384,384]{2,1,0:T(8,128)(2,1)} async-done(((bf16[5,384,384]{2,1,0:T(8,128)(2,1)}), bf16[80,384,384]{2,1,0:T(8,128)(2,1)}) %all-gather.2.cloned.1.call-update) | async-done | bytes 23592976 | tf_op jit(solution)/shard_map/all_gather | solution.py:700
  268.9 13.1 %gather_matrices.1 = (bf16[768,768]{1,0:T(8,128)(2,1)S(1)}, bf16[768,2304]{1,0:T(8,128)(2,1)}, bf16[768,768]{1,0:T(8,128)(2,1)}, bf16[768,3072]{1,0:T(8,128)(2,1...) custom-call(s32[68]{0:T(128)} %slots_ref.3, ...), custom_call_target="tpu_custom_call" | custom-call | tf_op jit(solution)/shard_map/gather_matrices/pallas_call | solution.py:556
  282.1 51.6 %conditional.3 = (bf16[2,128,768]{2,1,0:T(8,128)(2,1)}, f32[2,128,768]{2,1,0:T(8,128)S(1)}, f32[2,128,768]{2,1,0:T(8,128)S(1)}, bf16[2,128,768]{2,1,0:T(8,128)(2...) conditional(s32[]{:T(128)} %convert_element_type.488, ...), branch_computations={%region_0.11_spmd, %region_11.20_spmd} | conditional | flops 6889146368 | bytes 112085792 | solution.py:755
  290.5 3.2 fusion.338
  306.4 11.5 fusion.11
  324.2 3.1 copy.430
  333.8 23.2 %collective-permute-start = (bf16[2,128,768]{2,1,0:T(8,128)(2,1)}, bf16[2,128,768]{2,1,0:T(8,128)(2,1)S(1)}, u32[]{:S(2)}, u32[]{:S(2)}) collective-permute-start(bf16[2,128,768]{2,1,0:T(8,128)(2,1)} %get-tuple-element.344), channel_id=1, source_target_pairs={{0,16},{1,17},{2,18},{3,19},{4,20},{5,21},{6,22},{7,23},{8,24},{9,... | collective-permute-start | bytes 1179656 | tf_op jit(solution)/shard_map/ppermute | solution.py:50
  363.4 19.8 %conditional.4 = (bf16[2,128,768]{2,1,0:T(8,128)(2,1)S(1)}, f32[384,1152]{1,0:T(8,128)}, f32[384,384]{1,0:T(8,128)S(1)}, f32[384,1536]{1,0:T(8,128)}, f32[1536,3...) conditional(s32[]{:T(128)} %convert_element_type.488, ...), branch_computations={%region_20.50_spmd, %region_50.51_spmd} | conditional | flops 8059757056 | bytes 305179552 | solution.py:782
  427.2 122.8 %collective-permute-done.1 = bf16[2,128,768]{2,1,0:T(8,128)(2,1)S(1)} collective-permute-done((bf16[2,128,768]{2,1,0:T(8,128)(2,1)S(1)}, bf16[2,128,768]{2,1,0:T(8,128)(2,1)S(1)}, u32[]{:S(2)}, u32[]{:S(2)}) %collective-permute-start.1) | collective-permute-done | bytes 393248 | tf_op jit(solution)/shard_map/ppermute | solution.py:50
  550.0 98.7 %conditional.5 = (f32[768,768]{0,1:T(8,128)}, f32[768,2304]{0,1:T(8,128)}, f32[768,768]{0,1:T(8,128)}, f32[768,3072]{0,1:T(8,128)}, f32[3072,768]{0,1:T(8,128)}, /*index=5*/f32[11520]{0:T(1024)}) conditional(s32[]{:T(128)} %convert_element_type.488, () %tuple.36, (f32[2,128,3072]{2,1,0:T(8,128)}, bf16[2,128,768]{2,1,0:T(8,128)(2,1)S(1)}, ...), branch_computations={%region_51.52_spmd, %region_52.77_spmd} | conditional | flops 7836194816 | bytes 147070736 | solution.py:803
  553.0 21.9 %fusion.345 = (f32[3072]{0:T(1024)}, bf16[2,128,3072]{2,1,0:T(8,128)(2,1)}) fusion(f32[2,128,3072]{2,1,0:T(8,128)} %get-tuple-element.253, bf16[3072,768]{1,0:T(8,128)(2,1)} %get-tuple-element.257, f32[2,128,768]{2,1,0:T(8,128)S(1)} %get-tuple-element.856, f32[2,128]{1,0:T(2,128)S(1)} %negate_multiply_fusion.4), kind=kOutput, calls=%fused_computation.731 | convolution fusion | flops 1265759232 | bytes 10236928 | tf_op jit(solution)/shard_map/cond/branch_1_fun/...m,km->...k/dot_general | solution.py:111
  575.1 4.9 multiply_reduce_fusion.9
  583.3 3.2 copy.467
  603.1 4.0 multiply_reduce_fusion.5
  626.9 4.0 convolution_bitcast_fusion.2
  635.8 6.1 convolution_bitcast_fusion.1
  641.9 6.5 convolution_bitcast_fusion
  648.8 9.6 copy.476
  658.4 5.0 abs_reduce_fusion
  663.4 5.0 abs_reduce_fusion.1
  668.4 9.6 copy.474
  678.0 3.0 copy.473
  683.5 4.1 abs_reduce_fusion.2
  687.6 8.0 copy.471
  698.0 3.0 copy.470
  701.8 4.5 multiply_convert_fusion.3
  709.3 3.4 collective-permute-start.25
  719.7 4.4 multiply_convert_fusion.4
  730.3 7.0 collective-permute-done.3
  740.4 3.4 collective-permute-start.7
  753.5 3.4 collective-permute-start.5
  759.0 3.3 collective-permute-start.23
  765.5 3.4 collective-permute-start.20
  788.3 4.0 collective-permute-start.29
  794.7 4.0 collective-permute-start.11
  806.4 3.3 collective-permute-start.12
  815.8 9.1 collective-permute-done.2
  827.5 15.6 %collective-permute-done.17 = f16[192,768]{1,0:T(8,128)(2,1)S(1)} collective-permute-done((f16[192,768]{1,0:T(8,128)(2,1)S(1)}, f16[192,768]{1,0:T(8,128)(2,1)S(1)}, u32[]{:S(2)}, u32[]{:S(2)}) %collective-permute-start.17) | collective-permute-done | bytes 294944 | tf_op jit(solution)/shard_map/ppermute | solution.py:617
  843.2 3.3 collective-permute-start.4
  846.6 5.1 collective-permute-done.4
  855.7 4.0 collective-permute-done.18
  862.6 4.1 collective-permute-done.6
  867.5 4.0 collective-permute-start.10
  875.5 3.2 collective-permute-start.19
  878.7 4.3 collective-permute-done.19
  893.1 4.2 convert_multiply_fusion.2
  897.4 3.3 bitcast_add_fusion
  909.4 3.4 collective-permute-start.22
  914.6 3.4 collective-permute-start.14
  920.0 5.1 collective-permute-done.14
  926.0 4.4 collective-permute-start.15
  931.2 6.2 collective-permute-done.15
  948.8 3.4 collective-permute-start.24
  952.1 3.9 collective-permute-done.32
  956.5 3.8 collective-permute-start.33
  962.8 3.8 collective-permute-start.28
  969.3 6.1 collective-permute-done.28
  981.3 6.1 all-to-all-start
  1002.5 5.4 collective-permute-start.55
  1023.2 42.2 %soap_first.1 = (f32[5,384,384]{2,1,0:T(8,128)}, f32[5,384,384]{2,1,0:T(8,128)}, f32[5,384,384]{2,1,0:T(8,128)}, f32[5,384,384]{2,1,0:T(8,128)}, f32[5,384,384]{...) custom-call(s32[5]{0:T(128)} %get-tuple-element.960.flag, f32[1]{0:T(128)} %bitcast.238.factor, ...), custom_call_target="tpu_custom_call" | custom-call | tf_op jit(solution)/shard_map/soap_first/pallas_call | solution.py:473
  1065.4 3.2 convert_element_type.584
  1073.5 64.2 %soap_factor.1.q_ref = f32[5,2,384,384]{3,2,1,0:T(8,128)} custom-call(s32[5]{0:T(128)} %get-tuple-element.960.flag, f32[5,2,384,384]{3,2,1,0:T(8,128)} %get-tuple-element.381.base_ref, f32[5,2,384,384]{3,2,1,0:T(8,128)} %get-tuple-element.382.gram_ref), custom_call_target="tpu_custom_call" | custom-call | tf_op jit(solution)/shard_map/soap_factor/pallas_call | solution.py:487
  1137.7 14.5 %soap_last.1 = (f32[5,384,384]{2,1,0:T(8,128)}, f32[5,384,384]{2,1,0:T(8,128)}, f32[5,384,384]{2,1,0:T(8,128)}) custom-call(s32[5]{0:T(128)} %get-tuple-element.960.flag, f32[5,384,384]{2,1,0:T(8,128)} %bitcast.576, f32[5,384,384]{2,1,0:T(8,128)} %bitcast.578, f32[5,384,384]{2,1,0:T(8,128)} %get-tuple-element.380.m_ref, f32[5,2,384,384]{3,2,1,0:T(8,128)} %soap_factor.1.q_ref), custom_call_target="tpu_custom_call" | custom-call | tf_op jit(solution)/shard_map/soap_last/pallas_call | solution.py:510
  (606 shorter events, 270.5 us)
Async XLA Ops:
  7.2 261.7 %all-gather.2.cloned.1.call-start = ((), (), s32[]{:S(2)}) async-start(), calls=%async_computation.1 | async-start | bytes 25067520 | tf_op jit(solution)/shard_map/all_gather | solution.py:700
  10.6 271.5 %copy-start.104 = (s32[2,4,36]{2,1,0:T(4,128)}, s32[2,4,36]{2,1,0:T(4,128)S(1)}, u32[]{:S(2)}) copy-start(s32[2,4,36]{2,1,0:T(4,128)S(1)} %lt.180) | copy-start | bytes 3460
  10.9 271.2 %copy-start.90 = (f32[768]{0:T(1024)}, f32[768]{0:T(1024)S(1)}, u32[]{:S(2)}) copy-start(f32[768]{0:T(1024)S(1)} %get-tuple-element.844) | copy-start | bytes 9220
  10.9 271.2 %copy-start.100 = (f32[768]{0:T(1024)}, f32[768]{0:T(1024)S(1)}, u32[]{:S(2)}) copy-start(f32[768]{0:T(1024)S(1)} %get-tuple-element.849) | copy-start | bytes 9220
  333.8 29.6 %collective-permute-start = (bf16[2,128,768]{2,1,0:T(8,128)(2,1)}, bf16[2,128,768]{2,1,0:T(8,128)(2,1)S(1)}, u32[]{:S(2)}, u32[]{:S(2)}) collective-permute-start(bf16[2,128,768]{2,1,0:T(8,128)(2,1)} %get-tuple-element.344), channel_id=1, source_target_pairs={{0,16},{1,17},{2,18},{3,19},{4,20},{5,21},{6,22},{7,23},{8,24},{9,... | collective-permute-start | bytes 1179656 | tf_op jit(solution)/shard_map/ppermute | solution.py:50
  392.1 414.3 %collective-permute-start.34 = (f16[1152,384]{1,0:T(8,128)(2,1)}, f16[1152,384]{1,0:T(8,128)(2,1)}, u32[]{:S(2)}, u32[]{:S(2)}) collective-permute-start(f16[1152,384]{1,0:T(8,128)(2,1)} %bitcast.190), channel_id=1, source_target_pairs={{16,18},{17,19},{18,16},{19,17},{20,22},{21,23},{22,20},{23,21},{2... | collective-permute-start | bytes 2654216 | tf_op jit(solution)/shard_map/ppermute | solution.py:617
  395.0 16.0 %collective-permute-start.35 = (f32[128]{0:T(128)}, f32[128]{0:T(128)S(1)}, u32[]{:S(2)}, u32[]{:S(2)}) collective-permute-start(f32[128]{0:T(128)} %pad.92), channel_id=1, source_target_pairs={{16,18},{17,19},{18,16},{19,17},{20,22},{21,23},{22,20},{23,21},{2... | collective-permute-start | bytes 1544 | tf_op jit(solution)/shard_map/ppermute | solution.py:617
  400.2 11.4 collective-permute-start.39
  407.9 459.6 %collective-permute-start.44 = (f16[192,3840]{1,0:T(8,128)(2,1)}, f16[192,3840]{1,0:T(8,128)(2,1)}, u32[]{:S(2)}, u32[]{:S(2)}) collective-permute-start(f16[192,3840]{1,0:T(8,128)(2,1)} %bitcast.218), channel_id=1, source_target_pairs={{16,17},{17,16},{18,19},{19,18},{20,21},{21,20},{22,23},{23,22},{2... | collective-permute-start | bytes 4423688 | tf_op jit(solution)/shard_map/ppermute | solution.py:617
  409.7 140.4 %collective-permute-start.1 = (bf16[2,128,768]{2,1,0:T(8,128)(2,1)S(1)}, bf16[2,128,768]{2,1,0:T(8,128)(2,1)S(1)}, u32[]{:S(2)}, u32[]{:S(2)}) collective-permute-start(bf16[2,128,768]{2,1,0:T(8,128)(2,1)S(1)} %copy-done.83), channel_id=1, source_target_pairs={{16,0},{17,1},{18,2},{19,3},{20,4},{21,5},{22,6},{23,7},{24,8},{25... | collective-permute-start | bytes 1179656 | tf_op jit(solution)/shard_map/ppermute | solution.py:50
  414.1 2.7 collective-permute-start.37
  415.3 1.6 collective-permute-start.40
  419.0 1.0 collective-permute-start.41
  424.0 1.0 collective-permute-start.43
  706.3 186.8 %collective-permute-start.30 = (f16[1536,768]{1,0:T(8,128)(2,1)}, f16[1536,768]{1,0:T(8,128)(2,1)}, u32[]{:S(2)}, u32[]{:S(2)}) collective-permute-start(f16[1536,768]{1,0:T(8,128)(2,1)} %bitcast.175), channel_id=1, source_target_pairs={{0,2},{1,3},{2,0},{3,1},{4,6},{5,7},{6,4},{7,5},{8,10},{9,11},{10,... | collective-permute-start | bytes 7077896 | tf_op jit(solution)/shard_map/ppermute | solution.py:617
  709.3 31.0 %collective-permute-start.25 = (f32[128]{0:T(128)S(1)}, f32[128]{0:T(128)S(1)}, u32[]{:S(2)}, u32[]{:S(2)}) collective-permute-start(f32[128]{0:T(128)S(1)} %pad.88), channel_id=1, source_target_pairs={{0,2},{1,3},{2,0},{3,1},{4,6},{5,7},{6,4},{7,5},{8,10},{9,11},{10,... | collective-permute-start | bytes 1544 | tf_op jit(solution)/shard_map/ppermute | solution.py:617
  716.3 21.0 %collective-permute-start.3 = (f32[128]{0:T(128)S(1)}, f32[128]{0:T(128)S(1)}, u32[]{:S(2)}, u32[]{:S(2)}) collective-permute-start(f32[128]{0:T(128)S(1)} %select_maximum_fusion.7), channel_id=1, source_target_pairs={{0,2},{1,3},{2,0},{3,1},{4,6},{5,7},{6,4},{7,5},{8,10},{9,11},{10,... | collective-permute-start | bytes 1544 | tf_op jit(solution)/shard_map/ppermute | solution.py:617
  737.3 7.0 collective-permute-start.21
  740.4 6.6 collective-permute-start.7
  749.8 13.1 %collective-permute-start.26 = (f32[128]{0:T(128)S(1)}, f32[128]{0:T(128)S(1)}, u32[]{:S(2)}, u32[]{:S(2)}) collective-permute-start(f32[128]{0:T(128)S(1)} %pad.89), channel_id=1, source_target_pairs={{0,1},{1,0},{2,3},{3,2},{4,5},{5,4},{6,7},{7,6},{8,9},{9,8},{10,11... | collective-permute-start | bytes 1544 | tf_op jit(solution)/shard_map/ppermute | solution.py:617
  753.5 5.5 collective-permute-start.5
  759.0 6.5 collective-permute-start.23
  762.9 8.3 collective-permute-start.8
  765.5 139.4 %collective-permute-start.20 = (f16[384,3072]{1,0:T(8,128)(2,1)}, f16[384,3072]{1,0:T(8,128)(2,1)}, u32[]{:S(2)}, u32[]{:S(2)}) collective-permute-start(f16[384,3072]{1,0:T(8,128)(2,1)} %bitcast.640), channel_id=1, source_target_pairs={{0,1},{1,0},{2,3},{3,2},{4,5},{5,4},{6,7},{7,6},{8,9},{9,8},{10,11... | collective-permute-start | bytes 7077896 | tf_op jit(solution)/shard_map/ppermute | solution.py:617
  772.9 5.4 collective-permute-start.27
  778.3 5.4 collective-permute-start.9
  788.3 6.3 collective-permute-start.29
  794.7 6.3 collective-permute-start.11
  801.0 12.0 %collective-permute-start.16 = (f16[384,768]{1,0:T(8,128)(2,1)}, f16[384,768]{1,0:T(8,128)(2,1)S(1)}, u32[]{:S(2)}, u32[]{:S(2)}) collective-permute-start(f16[384,768]{1,0:T(8,128)(2,1)} %bitcast.665), channel_id=1, source_target_pairs={{0,2},{1,3},{2,0},{3,1},{4,6},{5,7},{6,4},{7,5},{8,10},{9,11},{10,... | collective-permute-start | bytes 1769480 | tf_op jit(solution)/shard_map/ppermute | solution.py:617
  806.4 79.2 %collective-permute-start.12 = (f16[384,2304]{1,0:T(8,128)(2,1)}, f16[384,2304]{1,0:T(8,128)(2,1)S(1)}, u32[]{:S(2)}, u32[]{:S(2)}) collective-permute-start(f16[384,2304]{1,0:T(8,128)(2,1)} %bitcast.643), channel_id=1, source_target_pairs={{0,1},{1,0},{2,3},{3,2},{4,5},{5,4},{6,7},{7,6},{8,9},{9,8},{10,11... | collective-permute-start | bytes 5308424 | tf_op jit(solution)/shard_map/ppermute | solution.py:617
  813.0 12.0 %collective-permute-start.2 = (f16[384,768]{1,0:T(8,128)(2,1)S(1)}, f16[384,768]{1,0:T(8,128)(2,1)S(1)}, u32[]{:S(2)}, u32[]{:S(2)}) collective-permute-start(f16[384,768]{1,0:T(8,128)(2,1)S(1)} %bitcast.664), channel_id=1, source_target_pairs={{0,2},{1,3},{2,0},{3,1},{4,6},{5,7},{6,4},{7,5},{8,10},{9,11},{10,... | collective-permute-start | bytes 1769480 | tf_op jit(solution)/shard_map/ppermute | solution.py:617
  824.9 18.2 %collective-permute-start.17 = (f16[192,768]{1,0:T(8,128)(2,1)S(1)}, f16[192,768]{1,0:T(8,128)(2,1)S(1)}, u32[]{:S(2)}, u32[]{:S(2)}) collective-permute-start(f16[192,768]{1,0:T(8,128)(2,1)S(1)} %bitcast.681), channel_id=1, source_target_pairs={{0,1},{1,0},{2,3},{3,2},{4,5},{5,4},{6,7},{7,6},{8,9},{9,8},{10,11... | collective-permute-start | bytes 884744 | tf_op jit(solution)/shard_map/ppermute | solution.py:617
  843.2 8.6 collective-permute-start.4
  851.8 0.9 collective-permute-start.36
  852.7 7.0 collective-permute-start.18
  859.7 7.0 collective-permute-start.6
  866.8 17.1 %collective-permute-start.38 = (f16[288,384]{1,0:T(8,128)(2,1)S(1)}, f16[288,384]{1,0:T(8,128)(2,1)S(1)}, u32[]{:S(2)}, u32[]{:S(2)}) collective-permute-start(f16[288,384]{1,0:T(8,128)(2,1)S(1)} %bitcast.683), channel_id=1, source_target_pairs={{16,20},{17,21},{18,22},{19,23},{20,16},{21,17},{22,18},{23,19},{2... | collective-permute-start | bytes 663560 | tf_op jit(solution)/shard_map/ppermute | solution.py:617
  867.5 7.9 collective-permute-start.10
  875.5 7.6 collective-permute-start.19
  883.0 2.8 collective-permute-start.45
  884.0 1.5 collective-permute-start.42
  886.6 5.4 collective-permute-start.46
  889.5 23.3 %collective-permute-start.13 = (f16[192,2304]{1,0:T(8,128)(2,1)S(1)}, f16[192,2304]{1,0:T(8,128)(2,1)S(1)}, u32[]{:S(2)}, u32[]{:S(2)}) collective-permute-start(f16[192,2304]{1,0:T(8,128)(2,1)S(1)} %bitcast.657), channel_id=1, source_target_pairs={{0,2},{1,3},{2,0},{3,1},{4,6},{5,7},{6,4},{7,5},{8,10},{9,11},{10,... | collective-permute-start | bytes 2654216 | tf_op jit(solution)/shard_map/ppermute | solution.py:617
  892.3 25.8 %collective-permute-start.47 = (f16[24,3840]{1,0:T(8,128)(2,1)S(1)}, f16[24,3840]{1,0:T(8,128)(2,1)S(1)}, u32[]{:S(2)}, u32[]{:S(2)}) collective-permute-start(f16[24,3840]{1,0:T(8,128)(2,1)S(1)} %fusion.283), channel_id=1, source_target_pairs={{16,24},{17,25},{18,26},{19,27},{20,28},{21,29},{22,30},{23,31},{2... | collective-permute-start | bytes 552968 | tf_op jit(solution)/shard_map/ppermute | solution.py:617
  902.0 38.6 %collective-permute-start.31 = (f16[768,768]{1,0:T(8,128)(2,1)}, f16[768,768]{1,0:T(8,128)(2,1)}, u32[]{:S(2)}, u32[]{:S(2)}) collective-permute-start(f16[768,768]{1,0:T(8,128)(2,1)} %bitcast.178), channel_id=1, source_target_pairs={{0,1},{1,0},{2,3},{3,2},{4,5},{5,4},{6,7},{7,6},{8,9},{9,8},{10,11... | collective-permute-start | bytes 3538952 | tf_op jit(solution)/shard_map/ppermute | solution.py:617
  909.4 37.4 %collective-permute-start.22 = (f16[192,3072]{1,0:T(8,128)(2,1)}, f16[192,3072]{1,0:T(8,128)(2,1)}, u32[]{:S(2)}, u32[]{:S(2)}) collective-permute-start(f16[192,3072]{1,0:T(8,128)(2,1)} %bitcast.152), channel_id=1, source_target_pairs={{0,2},{1,3},{2,0},{3,1},{4,6},{5,7},{6,4},{7,5},{8,10},{9,11},{10,... | collective-permute-start | bytes 3538952 | tf_op jit(solution)/shard_map/ppermute | solution.py:617
  914.6 10.4 collective-permute-start.14
  926.0 11.4 collective-permute-start.15
  944.3 11.8 %collective-permute-start.32 = (f16[384,768]{1,0:T(8,128)(2,1)S(1)}, f16[384,768]{1,0:T(8,128)(2,1)S(1)}, u32[]{:S(2)}, u32[]{:S(2)}) collective-permute-start(f16[384,768]{1,0:T(8,128)(2,1)S(1)} %bitcast.666), channel_id=1, source_target_pairs={{0,4},{1,5},{2,6},{3,7},{4,0},{5,1},{6,2},{7,3},{8,12},{9,13},{10,... | collective-permute-start | bytes 1769480 | tf_op jit(solution)/shard_map/ppermute | solution.py:617
  948.8 13.6 %collective-permute-start.24 = (f16[96,3072]{1,0:T(8,128)(2,1)S(1)}, f16[96,3072]{1,0:T(8,128)(2,1)S(1)}, u32[]{:S(2)}, u32[]{:S(2)}) collective-permute-start(f16[96,3072]{1,0:T(8,128)(2,1)S(1)} %bitcast.667), channel_id=1, source_target_pairs={{0,4},{1,5},{2,6},{3,7},{4,0},{5,1},{6,2},{7,3},{8,12},{9,13},{10,... | collective-permute-start | bytes 1769480 | tf_op jit(solution)/shard_map/ppermute | solution.py:617
  956.5 12.7 %collective-permute-start.33 = (f16[192,768]{1,0:T(8,128)(2,1)S(1)}, f16[192,768]{1,0:T(8,128)(2,1)S(1)}, u32[]{:S(2)}, u32[]{:S(2)}) collective-permute-start(f16[192,768]{1,0:T(8,128)(2,1)S(1)} %bitcast.679), channel_id=1, source_target_pairs={{0,8},{1,9},{2,10},{3,11},{4,12},{5,13},{6,14},{7,15},{8,0},{9,1},... | collective-permute-start | bytes 884744 | tf_op jit(solution)/shard_map/ppermute | solution.py:617
  962.8 12.7 %collective-permute-start.28 = (f16[48,3072]{1,0:T(8,128)(2,1)S(1)}, f16[48,3072]{1,0:T(8,128)(2,1)S(1)}, u32[]{:S(2)}, u32[]{:S(2)}) collective-permute-start(f16[48,3072]{1,0:T(8,128)(2,1)S(1)} %bitcast.680), channel_id=1, source_target_pairs={{0,8},{1,9},{2,10},{3,11},{4,12},{5,13},{6,14},{7,15},{8,0},{9,1},... | collective-permute-start | bytes 884744 | tf_op jit(solution)/shard_map/ppermute | solution.py:617
  981.3 39.4 %all-to-all-start = ((f16[16,128,384]{2,1,0:T(8,128)(2,1)}), f16[16,128,384]{2,1,0:T(8,128)(2,1)S(1)}, u32[]{:S(2)}, u32[]{:S(2)}) async-start(f16[16,128,384]{2,1,0:T(8,128)(2,1)} %concatenate.121), calls=%async_computation | async-start | bytes 3145728 | tf_op jit(solution)/shard_map/all_to_all | solution.py:841
  988.9 4.4 collective-permute-start.52
  993.3 5.0 collective-permute-start.53
  995.1 3.8 collective-permute-start.48
  998.4 4.2 collective-permute-start.54
  998.9 9.0 collective-permute-start.49
  1002.5 7.8 collective-permute-start.55
  1008.0 3.5 collective-permute-start.50
  1011.5 4.4 collective-permute-start.51
  1016.7 1.1 collective-permute-start.56
  1068.6 83.6 %collective-permute-start.57 = (bf16[5,384,384]{2,1,0:T(8,128)(2,1)}, bf16[5,384,384]{2,1,0:T(8,128)(2,1)S(1)}, u32[]{:S(2)}, u32[]{:S(2)}) collective-permute-start(bf16[5,384,384]{2,1,0:T(8,128)(2,1)} %convert_element_type.584), channel_id=1, source_target_pairs={{0,16},{1,17},{2,18},{3,19},{4,20},{5,21},{6,22},{7,23},{8,24},{9,... | collective-permute-start | bytes 4423688 | tf_op jit(solution)/shard_map/ppermute | solution.py:50
  1070.8 2.1 collective-permute-start.58
  (107 other events, 1940.4 us)
Sparse Core Ops, SparseCore 0:
  11.4 257.4 all-gather.1
